TPU v7x, 256 devices: a whole 4x4x8 slice. The times are simulated.
256 devices in a mesh: lat: 32 (over z, y_hi, core), lon: 8 (over y_lo, x).
Axes of the slice: x: 4, y: 4 (y_hi: 2, y_lo: 2; y = y_hi * 2 + y_lo), z: 8, core: 2. Of those that a mesh axis runs over, the one named last changes fastest.
Arguments:
- state_field: bfloat16 [73, 256, 1024], P(None, 'lat', 'lon'), may hold values from -6 to 6
- support_rows: int32 [128, 5], P('lat'), may hold values from -2 to 2, as said below
- window_bands: int32 [32], replicated, may hold values from 0 to 127, as said below
- conv_weight: bfloat16 [5, 3, 73, 256], replicated, may hold values from -0.1875 to 0.1875
- w_query: bfloat16 [256, 256], replicated
- w_key: bfloat16 [256, 256], replicated
- w_value: bfloat16 [256, 256], replicated, may hold values from -0.375 to 0.375
- w_out: bfloat16 [256, 256], replicated, may hold values from -0.75 to 0.75
Outputs:
- window_out: bfloat16 [32, 512, 256], P('lat', 'lon')
Inputs may be any that keep to these rules, and one draw needn't show every extreme that they name: `support_rows`: each row is a permutation of the 5 offsets from -2 to 2. `window_bands`: 32 distinct token bands.
All inputs are finite; a program needn't handle non-finite values.
Results may differ from a plain program's by a relative error of at most 0.019.
Values may be sent and summed in bfloat16 or wider, within the bound.
A program may use at most 64 MiB of HBM per device.

v0:
```python
import math

import jax
import jax.numpy as jnp
from jax import lax
from jax.sharding import PartitionSpec as P

D = 256
H = 4


def padded(x, sides, width):
    for axis, dim in sides:
        devices, length = (lax.axis_size(axis), x.shape[dim])
        up = [(i, (i + 1) % devices) for i in range(devices - 1)]
        down = [(j, i) for i, j in up]
        last = lax.slice_in_dim(x, length - width, length, axis=dim)
        leading = lax.slice_in_dim(x, 0, width, axis=dim)
        before = lax.ppermute(last, axis, up)
        after = lax.ppermute(leading, axis, down)
        x = jnp.concatenate([before, x, after], axis=dim)
    return x


def shifted(x, axis, by):
    devices = lax.axis_size(axis)
    return lax.ppermute(x, axis, [(i, (i + by) % devices) for i in range(devices)])


def conv_features(extended, support_rows, conv_weight):
    bands = support_rows.shape[0]
    width = (extended.shape[2] - 1) // 2
    row_index = 2 * jnp.arange(bands, dtype=jnp.int32)[:, None] + support_rows + 2
    picked = jnp.take(extended, row_index, axis=1)
    tapped = jnp.stack(
        [picked[..., column_tap : column_tap + 2 * width : 2] for column_tap in range(3)], axis=3
    )
    patches = jnp.transpose(tapped, (1, 4, 2, 3, 0)).reshape(bands * width, -1)
    raw = jnp.dot(
        patches, conv_weight.reshape(-1, conv_weight.shape[-1]), preferred_element_type=jnp.float32
    )
    factor = lax.rsqrt(jnp.mean(raw * raw, axis=-1, keepdims=True) + 1e-06)
    return (raw * factor).astype(jnp.bfloat16).reshape(bands, width, -1)


def absorb(carry, block_keys, block_values, block_area, queries, scale):
    running_max, running_sum, mixed = carry
    scores = (
        jnp.einsum("qhd,khd->qhk", queries, block_keys, preferred_element_type=jnp.float32) * scale
        + block_area
    )
    new_max = jnp.maximum(running_max, jnp.max(scores, axis=-1))
    factor = jnp.exp(running_max - new_max)
    weights = jnp.exp(scores - new_max[..., None])
    running_sum = running_sum * factor + jnp.sum(weights, axis=-1)
    update = jnp.einsum(
        "qhk,khd->qhd",
        weights.astype(jnp.bfloat16),
        block_values,
        preferred_element_type=jnp.float32,
    )
    mixed = mixed * factor[..., None] + update
    return (new_max, running_sum, mixed)


def sweep(carry, keys, values, queries, band_total):
    rows = keys.shape[0]
    lon_tile = keys.shape[1]
    head_size = D // H
    band_block = math.gcd(rows, max(1, 512 // lon_tile))
    blocks = rows // band_block
    block_len = band_block * lon_tile
    keys_blocks = keys.reshape(blocks, block_len, H, head_size)
    values_blocks = values.reshape(blocks, block_len, H, head_size)
    band_index = jnp.arange(rows, dtype=jnp.int32).astype(jnp.float32)
    centre = (band_index + 0.5) * (math.pi / band_total) - math.pi / 2
    area_rows = jnp.repeat(jnp.log(jnp.cos(centre)), lon_tile).reshape(blocks, block_len)
    scale = 1.0 / math.sqrt(head_size)

    def step_block(state, inputs):
        return (absorb(state, inputs[0], inputs[1], inputs[2], queries, scale), None)

    result, unused = lax.scan(step_block, carry, (keys_blocks, values_blocks, area_rows))
    return result


def per_device(
    state_field, support_rows, window_bands, conv_weight, w_query, w_key, w_value, w_out
):
    lat_tile = support_rows.shape[0]
    lon_tile = state_field.shape[2] // 2
    whole_lon = lon_tile * lax.axis_size("lon")
    band_total = lat_tile * lax.axis_size("lat")
    head_size = D // H
    extended = padded(state_field, (("lat", 1),), 2)
    western = shifted(extended[:, :, -1:], "lon", 1)
    extended = jnp.concatenate([western, extended], axis=2)
    features = conv_features(extended, support_rows, conv_weight)
    flat = features.reshape(-1, D)
    slot_count = window_bands.shape[0] // lax.axis_size("lat")
    local_queries = jnp.dot(flat, w_query, preferred_element_type=jnp.float32).astype(jnp.bfloat16)
    local_queries = local_queries.reshape(lat_tile, lon_tile * D)
    first_band = lax.axis_index("lat") * lat_tile
    wanted = window_bands - first_band
    onehot = (wanted[:, None] == jnp.arange(lat_tile, dtype=jnp.int32)[None, :]).astype(
        jnp.bfloat16
    )
    picked = jnp.dot(onehot, local_queries, preferred_element_type=jnp.float32)
    picked = picked.astype(jnp.bfloat16).astype(jnp.float32)
    mine = lax.psum_scatter(
        picked.reshape(slot_count * lax.axis_size("lat"), lon_tile, D).astype(jnp.bfloat16),
        "lat",
        scatter_dimension=0,
        tiled=True,
    )
    gathered = lax.all_gather(mine, "lon", axis=1, tiled=True)
    query_count = slot_count * whole_lon
    queries = gathered.reshape(query_count, H, head_size)
    initial = (
        jnp.full((query_count, H), -1e30, jnp.float32),
        jnp.zeros((query_count, H), jnp.float32),
        jnp.zeros((query_count, H, head_size), jnp.float32),
    )
    keys_local = (
        jnp.dot(flat, w_key, preferred_element_type=jnp.float32)
        .astype(jnp.bfloat16)
        .reshape(lat_tile, lon_tile, D)
    )
    values_local = (
        jnp.dot(flat, w_value, preferred_element_type=jnp.float32)
        .astype(jnp.bfloat16)
        .reshape(lat_tile, lon_tile, D)
    )
    carry = sweep(
        initial,
        lax.all_gather(keys_local, "lat", axis=0, tiled=True),
        lax.all_gather(values_local, "lat", axis=0, tiled=True),
        queries,
        band_total,
    )
    running_max, running_sum, mixed = carry
    best = lax.pmax(running_max, "lon")
    factor = jnp.exp(running_max - best)
    scaled_mix = (mixed * factor[..., None]).reshape(slot_count, whole_lon, D)
    scaled_sum = (running_sum * factor).reshape(slot_count, whole_lon, H)
    mix_share, sum_share = (
        lax.psum_scatter(
            scaled_mix.astype(jnp.bfloat16), "lon", scatter_dimension=1, tiled=True
        ).astype(jnp.float32),
        lax.psum_scatter(
            scaled_sum.astype(jnp.bfloat16), "lon", scatter_dimension=1, tiled=True
        ).astype(jnp.float32),
    )
    attended = mix_share.reshape(slot_count, lon_tile, H, head_size) / sum_share[..., None]
    attended = attended.astype(jnp.bfloat16).reshape(slot_count * lon_tile, D)
    result = jnp.dot(attended, w_out, preferred_element_type=jnp.float32).astype(jnp.bfloat16)
    return result.reshape(slot_count, lon_tile, D)


def solution(mesh):
    return jax.shard_map(
        per_device,
        mesh=mesh,
        in_specs=(P(None, "lat", "lon"), P("lat", None), P(), P(), P(), P(), P(), P()),
        out_specs=P("lat", "lon", None),
        check_vma=False,
    )
```

profile of v0, /device:TPU:1, one launch (start us, length us, event | category | flops | bytes accessed | tf_op | source)
XLA Modules:
  0.0 600.7 jit_solution(1551652999318973012)
XLA Ops:
  7.7 6.2 %collective-permute-start = (bf16[73,2,128]{0,2,1:T(8,128)(2,1)S(1)}, bf16[73,2,128]{0,2,1:T(8,128)(2,1)S(1)}, u32[]{:S(2)}, u32[]{:S(2)}) collective-permute-start(bf16[73,2,128]{0,2,1:T(8,128)(2,1)S(1)} %get-tuple-element.119), channel_id=1, source_target_pairs={{0,8},{8,16},{16,24},{24,32},{32,40},{40,48},{48,56},{56,64},{64,7... | collective-permute-start | bytes 112136 | tf_op jit(solution)/shard_map/ppermute | solution.py:19
  17.4 3.6 collective-permute-done.1
  23.6 2.1 collective-permute-done.2
  37.9 109.0 %reduce-scatter.8.cloned.1.call-done = bf16[1,64,256]{2,1,0:T(8,128)(2,1)} async-done(((bf16[32,64,256]{2,1,0:T(8,128)(2,1)}), bf16[1,64,256]{2,1,0:T(8,128)(2,1)}) %reduce-scatter.8.cloned.1.call-update) | async-done | bytes 32784 | tf_op jit(solution)/shard_map/reduce_scatter | solution.py:110
  146.9 22.4 %all_gather.10 = bf16[1,512,256]{2,1,0:T(8,128)(2,1)S(1)} all-gather(bf16[1,64,256]{2,1,0:T(8,128)(2,1)} %reduce-scatter.8.cloned.1.call-done), channel_id=1, replica_groups=mesh['lat'=32,'lon'=8] {'lon'}, dimensions={1}, use_global_device_ids=true | all-gather | bytes 294912 | tf_op jit(solution)/shard_map/all_gather | solution.py:116
  169.5 70.5 %all-gather.3.cloned.1.call-done = bf16[128,64,256]{2,1,0:T(8,128)(2,1)} async-done(((bf16[4,64,256]{2,1,0:T(8,128)(2,1)}), bf16[128,64,256]{2,1,0:T(8,128)(2,1)}) %all-gather.3.cloned.1.call-update) | async-done | bytes 4194320 | tf_op jit(solution)/shard_map/all_gather | solution.py:136
  239.9 12.9 %reshape.113 = bf16[16,512,4,64]{3,2,1,0:T(4,128)(2,1)} reshape(bf16[128,64,256]{2,1,0:T(8,128)(2,1)} %all-gather.3.cloned.1.call-done) | data formatting | bytes 8388608 | tf_op jit(solution)/shard_map/reshape | solution.py:73
  252.9 12.7 %copy.29 = bf16[16,512,4,64]{1,3,2,0:T(8,128)(2,1)} copy(bf16[16,512,4,64]{3,2,1,0:T(4,128)(2,1)} %reshape.113) | data formatting | bytes 8388608
  265.6 60.5 %all-gather.5.cloned.1.call-done = bf16[128,64,256]{2,1,0:T(8,128)(2,1)} async-done(((bf16[4,64,256]{2,1,0:T(8,128)(2,1)}), bf16[128,64,256]{2,1,0:T(8,128)(2,1)}) %all-gather.5.cloned.1.call-update) | async-done | bytes 4194320 | tf_op jit(solution)/shard_map/all_gather | solution.py:137
  326.1 12.9 %reshape.114 = bf16[16,512,4,64]{3,2,1,0:T(4,128)(2,1)} reshape(bf16[128,64,256]{2,1,0:T(8,128)(2,1)} %all-gather.5.cloned.1.call-done) | data formatting | bytes 8388608 | tf_op jit(solution)/shard_map/reshape | solution.py:74
  339.0 12.7 %copy.30 = bf16[16,512,4,64]{1,3,2,0:T(8,128)(2,1)} copy(bf16[16,512,4,64]{3,2,1,0:T(4,128)(2,1)} %reshape.114) | data formatting | bytes 8388608
  351.7 150.0 %while.15 = (s32[]{:T(128)}, f32[512,4]{0,1:T(4,128)S(1)}, f32[512,4]{0,1:T(4,128)S(1)}, f32[512,4,64]{0,2,1:T(8,128)S(1)}, bf16[16,512,4,64]{1,3,2,0:T(8,128)(2...) while((s32[]{:T(128)}, f32[512,4]{0,1:T(4,128)S(1)}, ...), condition=%wide.region_5.6_spmd.clone, body=%wide.region_2.0_spmd.clone.sunk | while | flops 280373248 | bytes 31337616 | solution.py:83
  351.7 3.8 bitcast_reduce_fusion.2
  355.5 3.2 fusion.46
  361.1 3.8 bitcast_reduce_fusion.2
  364.9 3.2 fusion.46
  370.5 3.8 bitcast_reduce_fusion.2
  374.3 3.2 fusion.46
  377.7 2.1 fusion.48
  379.8 3.8 bitcast_reduce_fusion.2
  383.7 3.2 fusion.46
  389.2 3.8 bitcast_reduce_fusion.2
  393.0 3.2 fusion.46
  398.6 3.8 bitcast_reduce_fusion.2
  402.4 3.2 fusion.46
  408.0 3.8 bitcast_reduce_fusion.2
  411.8 3.2 fusion.46
  417.3 3.8 bitcast_reduce_fusion.2
  421.1 3.2 fusion.46
  426.7 3.8 bitcast_reduce_fusion.2
  430.5 3.2 fusion.46
  436.1 3.8 bitcast_reduce_fusion.2
  439.9 3.2 fusion.46
  445.5 3.8 bitcast_reduce_fusion.2
  449.3 3.2 fusion.46
  454.8 3.8 bitcast_reduce_fusion.2
  458.6 3.2 fusion.46
  464.2 3.8 bitcast_reduce_fusion.2
  468.0 3.2 fusion.46
  473.6 3.8 bitcast_reduce_fusion.2
  477.4 3.2 fusion.46
  482.9 3.8 bitcast_reduce_fusion.2
  486.8 3.2 fusion.46
  492.3 3.8 bitcast_reduce_fusion.2
  496.1 3.2 fusion.46
  501.7 15.2 %pmax.7 = f32[512,4]{0,1:T(4,128)S(1)} all-reduce(f32[512,4]{0,1:T(4,128)S(1)} %get-tuple-element.50), channel_id=1, replica_groups=mesh['lat'=32,'lon'=8] {'lon'}, use_global_device_ids=true, to_apply=%region_6.7 | all-reduce | flops 2048 | bytes 16384 | tf_op jit(solution)/shard_map/pmax | solution.py:142
  519.0 32.0 %reduce-scatter.12.cloned.1.call-done = bf16[64,4]{1,0:T(8,128)(2,1)} async-done(((bf16[512,4]{1,0:T(8,128)(2,1)}), bf16[64,4]{1,0:T(8,128)(2,1)}) %reduce-scatter.12.cloned.1.call-update) | async-done | bytes 528
  551.9 40.5 %reduce-scatter.10.cloned.1.call-done = bf16[64,256]{1,0:T(8,128)(2,1)} async-done(((bf16[512,256]{1,0:T(8,128)(2,1)}), bf16[64,256]{1,0:T(8,128)(2,1)}) %reduce-scatter.10.cloned.1.call-update) | async-done | bytes 32784
  (179 shorter events, 58.6 us)
Async XLA Ops:
  6.5 27.1 %copy-start = (bf16[256,256]{1,0:T(8,128)(2,1)S(1)}, bf16[256,256]{1,0:T(8,128)(2,1)}, u32[]{:S(2)}) copy-start(bf16[256,256]{1,0:T(8,128)(2,1)} %param.14) | copy-start | bytes 393220
  6.5 140.3 %reduce-scatter.8.cloned.1.call-start = ((), (), s32[]{:S(2)}) async-start(), calls=%async_computation.4 | async-start | bytes 1081344 | tf_op jit(solution)/shard_map/reduce_scatter | solution.py:110
  7.7 9.7 %collective-permute-start = (bf16[73,2,128]{0,2,1:T(8,128)(2,1)S(1)}, bf16[73,2,128]{0,2,1:T(8,128)(2,1)S(1)}, u32[]{:S(2)}, u32[]{:S(2)}) collective-permute-start(bf16[73,2,128]{0,2,1:T(8,128)(2,1)S(1)} %get-tuple-element.119), channel_id=1, source_target_pairs={{0,8},{8,16},{16,24},{24,32},{32,40},{40,48},{48,56},{56,64},{64,7... | collective-permute-start | bytes 112136 | tf_op jit(solution)/shard_map/ppermute | solution.py:19
  13.9 7.1 %collective-permute-start.1 = (bf16[73,2,128]{0,2,1:T(8,128)(2,1)S(1)}, bf16[73,2,128]{0,2,1:T(8,128)(2,1)S(1)}, u32[]{:S(2)}, u32[]{:S(2)}) collective-permute-start(bf16[73,2,128]{0,2,1:T(8,128)(2,1)S(1)} %get-tuple-element.120), channel_id=1, source_target_pairs={{8,0},{16,8},{24,16},{32,24},{40,32},{48,40},{56,48},{64,56},{72,6... | collective-permute-start | bytes 112136 | tf_op jit(solution)/shard_map/ppermute | solution.py:20
  21.0 4.7 collective-permute-start.2
  32.0 3.7 copy-start.2
  32.0 4.7 copy-start.3
  35.7 204.3 %all-gather.3.cloned.1.call-start = ((), (), s32[]{:S(2)}) async-start(), calls=%async_computation.3 | async-start | bytes 4325376 | tf_op jit(solution)/shard_map/all_gather | solution.py:136
  36.7 289.4 %all-gather.5.cloned.1.call-start = ((), (), s32[]{:S(2)}) async-start(), calls=%async_computation.5 | async-start | bytes 4325376 | tf_op jit(solution)/shard_map/all_gather | solution.py:137
  37.6 513.4 %reduce-scatter.12.cloned.1.call-start = ((), (), s32[]{:S(2)}) async-start(), calls=%async_computation.7 | async-start | bytes 147456
  351.7 241.7 %copy-start.4 = (bf16[256,256]{1,0:T(8,128)(2,1)S(1)}, bf16[256,256]{1,0:T(8,128)(2,1)}, u32[]{:S(2)}) copy-start(bf16[256,256]{1,0:T(8,128)(2,1)} %param.17) | copy-start | bytes 393220
  355.5 3.4 copy-start.1
  364.9 3.4 copy-start.1
  374.3 3.4 copy-start.1
  383.6 3.4 copy-start.1
  393.0 3.4 copy-start.1
  402.4 3.4 copy-start.1
  411.8 3.4 copy-start.1
  421.1 3.4 copy-start.1
  430.5 3.4 copy-start.1
  439.9 3.4 copy-start.1
  449.3 3.4 copy-start.1
  458.6 3.4 copy-start.1
  468.0 3.4 copy-start.1
  477.4 3.4 copy-start.1
  486.7 3.4 copy-start.1
  496.1 3.4 copy-start.1
  517.7 74.7 %reduce-scatter.10.cloned.1.call-start = ((), (), s32[]{:S(2)}) async-start(), calls=%async_computation.6 | async-start | bytes 294912
Sparse Core Ops, SparseCore 0:
  35.8 111.0 reduce-scatter.7
  149.7 90.2 all-gather.2
  242.7 83.2 all-gather.4
  517.9 33.1 reduce-scatter.11
  553.4 38.9 reduce-scatter.9
where the time goes:
time: 608 us; the launch traced here: 601 us
  waiting for transfers between devices  318 us (52%)
  matrix products  97.6 us (16%)
  local copies, waits for them, and re-layouts  69 us (11%)
  other arithmetic  54.4 us (9%)
  blocking collectives  37.6 us (6%)
  between operations  13.4 us (2%)
  starting transfers between devices  9.58 us (2%)
    reduce_scatter x1, waiting for transfers between devices, per_device(): lax.psum_scatter(picked.reshape(slot_count * lax.axis_size('lat'), lon_ti...  109 us
    unnamed x7, waiting for transfers between devices  72.6 us
    all_gather x1, waiting for transfers between devices, per_device(): lax.all_gather(keys_local, 'lat', axis=0, tiled=True)  70.5 us
    dot_general x16, matrix products, absorb(): jnp.einsum('qhd,khd->qhk', queries, block_keys, preferred_element_type=jn...  60.8 us
    all_gather x1, waiting for transfers between devices, per_device(): lax.all_gather(values_local, 'lat', axis=0, tiled=True)  60.5 us
    reduce_sum x16, other arithmetic, absorb(): running_sum = running_sum * factor + jnp.sum(weights, axis=-1)  51.8 us
    dot_general x16, matrix products, absorb(): jnp.einsum('qhk,khd->qhd', weights.astype(jnp.bfloat16), block_values, pr...  33.2 us
    unnamed x20, local copies, waits for them, and re-layouts  31.6 us
  transfers between devices with their start and end apart: 8, of which 7 were waited for; matrix products, arithmetic and copies ran while one was open for 5% of the time, Pallas kernels for 0%

commit v1 on v0

v1 whole, which is shorter than its diff:
```python
import functools
import math

import jax
import jax.numpy as jnp
import numpy as np
from jax import lax
from jax.experimental import pallas as pl
from jax.experimental.pallas import tpu as pltpu
from jax.sharding import PartitionSpec as P

D = 256
H = 4
UP = (4, 3)
DOWN = (3, 4)


def shifted(x, axis, by):
    devices = lax.axis_size(axis)
    return lax.ppermute(x, axis, [(i, (i + by) % devices) for i in range(devices)])


def padded(x, sides, width):
    for axis, dim in sides:
        devices, length = (lax.axis_size(axis), x.shape[dim])
        up = [(i, (i + 1) % devices) for i in range(devices - 1)]
        down = [(j, i) for i, j in up]
        last = lax.slice_in_dim(x, length - width, length, axis=dim)
        leading = lax.slice_in_dim(x, 0, width, axis=dim)
        before = lax.ppermute(last, axis, up)
        after = lax.ppermute(leading, axis, down)
        x = jnp.concatenate([before, x, after], axis=dim)
    return x


def conv_features(extended, support_rows, conv_weight):
    bands = support_rows.shape[0]
    width = (extended.shape[2] - 1) // 2
    row_index = 2 * jnp.arange(bands, dtype=jnp.int32)[:, None] + support_rows + 2
    picked = jnp.take(extended, row_index, axis=1)
    tapped = jnp.stack(
        [picked[..., column_tap : column_tap + 2 * width : 2] for column_tap in range(3)], axis=3
    )
    patches = jnp.transpose(tapped, (1, 4, 2, 3, 0)).reshape(bands * width, -1)
    raw = jnp.dot(
        patches, conv_weight.reshape(-1, conv_weight.shape[-1]), preferred_element_type=jnp.float32
    )
    factor = lax.rsqrt(jnp.mean(raw * raw, axis=-1, keepdims=True) + 1e-06)
    return (raw * factor).astype(jnp.bfloat16)


def remote(src, dst, send, recv, **where):
    return pltpu.make_async_remote_copy(
        src_ref=src, dst_ref=dst, send_sem=send, recv_sem=recv,
        device_id=where, device_id_type=pl.DeviceIdType.MESH)


def greet(peers):
    barrier = pltpu.get_barrier_semaphore()
    for peer in peers:
        pl.semaphore_signal(barrier, inc=1, device_id=peer, device_id_type=pl.DeviceIdType.MESH)
    pl.semaphore_wait(barrier, len(peers))


def gather_kernel(nz, nlon, bands, slot_ref, x_ref, g_ref, q_ref, pick, ysend, yrecv, usend, urecv, dsend, drecv,
                  csend, crecv, qsend, qrecv):
    lat = lax.axis_index("lat")
    lon = lax.axis_index("lon")
    z, yh, c = lat // 4, (lat // 2) % 2, lat % 2

    def at(zz, t, cc):
        side = yh if t == 0 else 1 - yh
        return ((zz + nz) % nz) * 4 + side * 2 + cc

    up, down, across, twin = at(z + 1, 0, c), at(z - 1, 0, c), at(z, 1, c), at(z, 0, 1 - c)
    around = [(lon + k) % nlon for k in range(1, nlon)]
    greet([{"lat": p} for p in (up, down, across, twin)] + [{"lon": p} for p in around])

    waits = []

    def block(index):
        return g_ref.at[pl.ds(index * bands, bands)]

    def source(index, mine):
        return x_ref if mine else block(index)

    def send(index, mine, sends, recvs, to):
        copy = remote(source(index, mine), block(index), sends, recvs, lat=to)
        copy.start()
        waits.append(copy)

    def arrive(index, sends, recvs, peer):
        remote(block(index), block(index), sends, recvs, lat=peer).wait_recv()

    def hop_up(t, s):
        send(at(z - (s - 1), t, c), t == 0 and s == 1, usend.at[t, s - 1], urecv.at[t, s - 1], up)

    def hop_down(t, s):
        send(at(z + (s - 1), t, c), t == 0 and s == 1, dsend.at[t, s - 1], drecv.at[t, s - 1], down)

    twins = []

    def share(dz, t):
        k = len(twins)
        twins.append((dz, t))
        send(at(z + dz, t, c), dz == 0 and t == 0, csend.at[k], crecv.at[k], twin)

    send(lat, True, ysend.at[0], yrecv.at[0], across)
    hop_up(0, 1)
    hop_down(0, 1)
    share(0, 0)
    g_ref[pl.ds(lat * bands, bands)] = x_ref[...]
    arrive(at(z, 1, c), ysend.at[0], yrecv.at[0], across)
    hop_up(1, 1)
    hop_down(1, 1)
    share(0, 1)
    for s in range(1, max(UP + DOWN) + 1):
        for t in range(2):
            if s <= UP[t]:
                arrive(at(z - s, t, c), usend.at[t, s - 1], urecv.at[t, s - 1], down)
                if s < UP[t]:
                    hop_up(t, s + 1)
                share(-s, t)
            if s <= DOWN[t]:
                arrive(at(z + s, t, c), dsend.at[t, s - 1], drecv.at[t, s - 1], up)
                if s < DOWN[t]:
                    hop_down(t, s + 1)
                share(s, t)
    for k, (dz, t) in enumerate(twins):
        arrive(at(z + dz, t, 1 - c), csend.at[k], crecv.at[k], twin)
    chosen = g_ref[slot_ref[lat]]
    pick[...] = chosen
    q_ref[lon] = chosen
    for copy in waits:
        copy.wait_send()
    copies = []
    for k, peer in enumerate(around):
        copy = remote(pick, q_ref.at[lon], qsend.at[k], qrecv.at[k], lon=peer)
        copy.start()
        copies.append(copy)
    for k in range(1, nlon):
        slot = (lon + nlon - k) % nlon
        remote(pick, q_ref.at[slot], qsend.at[k - 1], qrecv.at[k - 1], lon=slot).wait_recv()
    for copy in copies:
        copy.wait_send()


def gather(features, window_bands, bands):
    nlat, nlon = lax.axis_size("lat"), lax.axis_size("lon")
    per = features.shape[1]
    v = pl.BlockSpec(memory_space=pltpu.VMEM)
    dma = pltpu.SemaphoreType.DMA
    nz = nlat // 4
    return pl.pallas_call(
        functools.partial(gather_kernel, nz, nlon, bands),
        out_shape=(
            jax.ShapeDtypeStruct((nlat * bands, per, D), jnp.bfloat16),
            jax.ShapeDtypeStruct((nlon, per, D), jnp.bfloat16),
        ),
        in_specs=[pl.BlockSpec(memory_space=pltpu.SMEM), v],
        out_specs=(v, v),
        scratch_shapes=[
            pltpu.VMEM((per, D), jnp.bfloat16),
            dma((1,)), dma((1,)), dma((2, 4)), dma((2, 4)), dma((2, 4)), dma((2, 4)),
            dma((2 * nz,)), dma((2 * nz,)), dma((nlon - 1,)), dma((nlon - 1,)),
        ],
        compiler_params=pltpu.CompilerParams(collective_id=0, has_side_effects=True, vmem_limit_bytes=24 * 1024 * 1024),
        name="gather_features",
    )(window_bands, features)


def finish_kernel(nlon, o_ref, w_ref, out_ref, held, send, recv):
    lon = lax.axis_index("lon")
    around = [(lon + k) % nlon for k in range(1, nlon)]
    rows = o_ref.shape[0] // nlon
    greet([{"lon": p} for p in around])
    copies = []
    for k, peer in enumerate(around):
        part = o_ref.at[pl.ds(pl.multiple_of(peer * rows, rows), rows), :]
        copy = remote(part, held.at[lon], send.at[k], recv.at[k], lon=peer)
        copy.start()
        copies.append(copy)
    held[lon] = o_ref[pl.ds(pl.multiple_of(lon * rows, rows), rows), :]
    for k in range(1, nlon):
        slot = (lon + nlon - k) % nlon
        remote(held.at[slot], held.at[slot], send.at[k - 1], recv.at[k - 1], lon=slot).wait_recv()
    logs = []
    for i in range(nlon):
        tail = held[i, :, D : D + 128].astype(jnp.float32)
        logs.append([jnp.sum(tail[:, 3 * h : 3 * h + 3], axis=1, keepdims=True) for h in range(H)])
    head = lax.broadcasted_iota(jnp.int32, (rows, D), 1) // (D // H)
    top = [functools.reduce(jnp.maximum, [logs[i][h] for i in range(nlon)]) for h in range(H)]
    share = [[jnp.exp(logs[i][h] - top[h]) for h in range(H)] for i in range(nlon)]
    total = [1.0 / sum(share[i][h] for i in range(nlon)) for h in range(H)]
    mixed = jnp.zeros((rows, D), jnp.float32)
    for i in range(nlon):
        factor = jnp.zeros((rows, D), jnp.float32)
        for h in range(H):
            factor = jnp.where(head == h, share[i][h] * total[h], factor)
        mixed = mixed + factor * held[i, :, 0:D].astype(jnp.float32)
    out_ref[...] = jnp.dot(
        mixed.astype(jnp.bfloat16), w_ref[...], preferred_element_type=jnp.float32
    ).astype(jnp.bfloat16)
    for copy in copies:
        copy.wait_send()


def finish(partial, w_out):
    nlon = lax.axis_size("lon")
    rows = partial.shape[0] // nlon
    v = pl.BlockSpec(memory_space=pltpu.VMEM)
    dma = pltpu.SemaphoreType.DMA
    return pl.pallas_call(
        functools.partial(finish_kernel, nlon),
        out_shape=jax.ShapeDtypeStruct((rows, D), jnp.bfloat16),
        in_specs=[v, v],
        out_specs=v,
        scratch_shapes=[
            pltpu.VMEM((nlon, rows, partial.shape[1]), jnp.bfloat16),
            dma((nlon - 1,)), dma((nlon - 1,)),
        ],
        compiler_params=pltpu.CompilerParams(collective_id=1, has_side_effects=True),
        name="finish",
    )(partial, w_out)


def split3(x):
    a = x.astype(jnp.bfloat16)
    r = x - a.astype(jnp.float32)
    b = r.astype(jnp.bfloat16)
    c = (r - b.astype(jnp.float32)).astype(jnp.bfloat16)
    return a, b, c

def attn_kernel(bk, qc, f_ref, qf_ref, wq_ref, wkv_ref, area_ref, o_ref, ka, va, qa, acc, mx):
    nk = f_ref.shape[0]; nq = qf_ref.shape[0]
    per = nk // area_ref.shape[0]
    rows = 2 * nq
    pb = 512
    def prep(i, c):
        r = pl.ds(pl.multiple_of(i*pb, pb), pb)
        fb = f_ref[r, :]
        kv = jnp.dot(fb, wkv_ref[...], preferred_element_type=jnp.float32).astype(jnp.bfloat16)
        e = area_ref[pl.ds(pl.multiple_of(i*(pb//per), pb//per), pb//per), :]
        e = jnp.broadcast_to(e[:, None, :], (pb//per, per, 128)).reshape(pb, 128).astype(jnp.bfloat16)
        for p in range(2):
            ka[p, r, 0:128] = kv[:, p*128:(p+1)*128]
            ka[p, r, 128:256] = e
            va[p, r, 0:128] = kv[:, 256+p*128:256+(p+1)*128]
            va[p, r, 128:256] = e
        return c
    lax.fori_loop(0, nk//pb, prep, 0)
    q = jnp.dot(qf_ref[...], wq_ref[...], preferred_element_type=jnp.float32).astype(jnp.bfloat16).astype(jnp.float32) * 0.125
    lane = lax.broadcasted_iota(jnp.int32, (nq, 128), 1)
    for p in range(2):
        qp = q[:, p*128:(p+1)*128]
        qa[p, 0:nq, 0:128] = jnp.where(lane < 64, qp, 0.0).astype(jnp.bfloat16)
        qa[p, nq:rows, 0:128] = jnp.where(lane >= 64, qp, 0.0).astype(jnp.bfloat16)
    elane = lax.broadcasted_iota(jnp.int32, (rows, 128), 1)
    ones = jnp.where(elane < 3, 1.0, 0.0)

    def set_shift(p, m):
        a, b, c = split3(m)
        f = lambda t: t.astype(jnp.float32)
        e = ones - jnp.where(elane == 3, f(a), 0.0) - jnp.where(elane == 4, f(b), 0.0) - jnp.where(elane == 5, f(c), 0.0)
        qa[p, :, 128:256] = e.astype(jnp.bfloat16)

    for p in range(2):
        qa[p, :, 128:256] = ones.astype(jnp.bfloat16)
    def scores(p, qr, kr):
        return lax.dot_general(qa[p, qr, :], ka[p, kr, :], (((1,), (1,)), ((), ())), preferred_element_type=jnp.float32)

    sub = pl.ds(nk//2 - 256, 512)
    nqc = rows // qc
    for p in range(2):
        for j in range(rows // 256):
            mx[p, j*256:(j+1)*256, :] = jnp.broadcast_to(jnp.max(scores(p, pl.ds(j*256, 256), sub), axis=1, keepdims=True), (256, 128))
        set_shift(p, mx[p])

    def sweep():
        acc[...] = jnp.zeros_like(acc)
        def body(i, c):
            kr = pl.ds(pl.multiple_of(i*bk, bk), bk)
            for p in range(2):
                for j in range(nqc):
                    qr = pl.ds(j*qc, qc)
                    w = jnp.exp(scores(p, qr, kr)).astype(jnp.bfloat16)
                    acc[p, qr, :] += jnp.dot(w, va[p, kr, :], preferred_element_type=jnp.float32)
            return c
        lax.fori_loop(0, nk//bk, body, 0)
    sweep()
    worst = jnp.maximum(jnp.max(acc[0, :, 131:132]), jnp.max(acc[1, :, 131:132]))

    @pl.when(jnp.logical_not(worst < 1e30))
    def _():
        for p in range(2):
            qa[p, :, 128:256] = ones.astype(jnp.bfloat16)
        mx[...] = jnp.full_like(mx, -jnp.inf)
        def body(i, c):
            kr = pl.ds(pl.multiple_of(i*512, 512), 512)
            p = c
            for p in range(2):
                def qb(j, cc):
                    qr = pl.ds(pl.multiple_of(j*256, 256), 256)
                    s = jnp.max(scores(p, qr, kr), axis=1, keepdims=True)
                    mx[p, qr, :] = jnp.maximum(mx[p, qr, :], s)
                    return cc
                lax.fori_loop(0, rows//256, qb, 0)
            return c
        lax.fori_loop(0, nk//512, body, 0)
        for p in range(2):
            set_shift(p, mx[p])
        sweep()

    tail = jnp.zeros((nq, 128), jnp.float32)
    for p in range(2):
        la = acc[p, 0:nq, 131:132]; lb = acc[p, nq:rows, 131:132]
        o_ref[:, p*128:(p+1)*128] = jnp.where(lane < 64, acc[p, 0:nq, 0:128] / la, acc[p, nq:rows, 0:128] / lb).astype(jnp.bfloat16)
        for s, (l, off) in enumerate(((la, 0), (lb, nq))):
            lse = mx[p, off:off+nq, 0:1] + jnp.log(l)
            pieces = split3(lse)
            h = 2*p + s
            for t in range(3):
                tail = jnp.where(lane == 3*h + t, pieces[t].astype(jnp.float32), tail)
    o_ref[:, 256:384] = tail.astype(jnp.bfloat16)

def area_table(nlat):
    c = (np.arange(nlat, dtype=np.float64) + 0.5) * (math.pi / nlat) - math.pi/2
    a = np.log(np.cos(c)).astype(np.float32)
    t = np.zeros((nlat, 128), np.float32)
    hi = a.astype(jnp.bfloat16).astype(np.float32)
    r = a - hi; mid = r.astype(jnp.bfloat16).astype(np.float32)
    lo = (r-mid).astype(jnp.bfloat16).astype(np.float32)
    t[:,0]=hi; t[:,1]=mid; t[:,2]=lo; t[:,3:6]=1.0
    return t

def attention(f, qf, wq, wk, wv, nlat, bk=2048, qc=256):
    nk, nq = f.shape[0], qf.shape[0]
    wkv = jnp.concatenate([wk, wv], axis=1)
    v = pl.BlockSpec(memory_space=pltpu.VMEM)
    return pl.pallas_call(
        functools.partial(attn_kernel, bk, qc),
        out_shape=jax.ShapeDtypeStruct((nq, 384), jnp.bfloat16),
        in_specs=[v]*5, out_specs=v,
        scratch_shapes=[pltpu.VMEM((2, nk, 256), jnp.bfloat16), pltpu.VMEM((2, nk, 256), jnp.bfloat16),
            pltpu.VMEM((2, 2*nq, 256), jnp.bfloat16), pltpu.VMEM((2, 2*nq, 256), jnp.float32), pltpu.VMEM((2, 2*nq, 128), jnp.float32)],
        compiler_params=pltpu.CompilerParams(vmem_limit_bytes=40*1024*1024),
        name="attend",
    )(f, qf, wq, wkv, jnp.asarray(area_table(nlat)))


def per_device(
    state_field, support_rows, window_bands, conv_weight, w_query, w_key, w_value, w_out
):
    lat_tile = support_rows.shape[0]
    lon_tile = state_field.shape[2] // 2
    band_total = lat_tile * lax.axis_size("lat")
    extended = padded(state_field, (("lat", 1),), 2)
    western = shifted(extended[:, :, -1:], "lon", 1)
    extended = jnp.concatenate([western, extended], axis=2)
    features = conv_features(extended, support_rows, conv_weight)
    everything, chosen = gather(features.reshape(lat_tile, lon_tile, D), window_bands, lat_tile)
    partial = attention(
        everything.reshape(-1, D), chosen.reshape(-1, D), w_query, w_key, w_value, band_total
    )
    return finish(partial, w_out).reshape(1, lon_tile, D)


def solution(mesh):
    return jax.shard_map(
        per_device,
        mesh=mesh,
        in_specs=(P(None, "lat", "lon"), P("lat", None), P(), P(), P(), P(), P(), P()),
        out_specs=P("lat", "lon", None),
        check_vma=False,
    )
```

time: 608 us -> 171 us (0.28); the launches traced: 601 us -> 170 us
  waiting for transfers between devices: 318 us -> 6.5 us
  Pallas kernels: 0 us -> 141 us
  matrix products: 97.6 us -> 0.45 us
  local copies, waits for them, and re-layouts: 69 us -> 10.5 us
  other arithmetic: 54.4 us -> 2.4 us
  blocking collectives: 37.6 us -> 0 us
  between operations: 13.4 us -> 0.2 us
    pallas_call x0 -> x3, Pallas kernels: none -> 141 us  [the longest x1 88.8 us: attention(): pl.pallas_call(functools.partial(attn_kernel, bk, qc), out_shape=jax.Shap...]
    all_gather x2 -> x0, waiting for transfers between devices: 131 us -> none  [the longest x1 70.5 us: per_device(): lax.all_gather(keys_local, 'lat', axis=0, tiled=True)]
    reduce_scatter x1 -> x0, waiting for transfers between devices: 109 us -> none  [per_device(): lax.psum_scatter(picked.reshape(slot_count * lax.axis_size('lat'), lon_ti...]
    dot_general x37 -> x0, matrix products: 97.2 us -> none  [the longest x16 60.8 us: absorb(): jnp.einsum('qhd,khd->qhk', queries, block_keys, preferred_element_type=jn...]
    unnamed x7 -> x0, waiting for transfers between devices: 72.6 us -> none
    reduce_sum x16 -> x0, other arithmetic: 51.8 us -> none  [absorb(): running_sum = running_sum * factor + jnp.sum(weights, axis=-1)]
    unnamed x20 -> x12, local copies, waits for them, and re-layouts: 31.6 us -> 3.34 us
    reshape x3 -> x0, local copies, waits for them, and re-layouts: 25.9 us -> none  [the longest x1 12.9 us: sweep(): keys_blocks = keys.reshape(blocks, block_len, H, head_size)]
  transfers between devices with their start and end apart: 8 -> 3, of which waited for: 7 -> 2; matrix products, arithmetic and copies ran while one was open for 5% -> 1% of each run, Pallas kernels for 0% -> 0%
where the time goes in v1:
time: 171 us; the launch traced here: 170 us
  Pallas kernels  141 us (82%)
  local copies, waits for them, and re-layouts  10.5 us (6%)
  starting transfers between devices  9.41 us (6%)
  waiting for transfers between devices  6.5 us (4%)
  other arithmetic  2.4 us (1%)
    pallas_call x1, Pallas kernels, attention(): pl.pallas_call(functools.partial(attn_kernel, bk, qc), out_shape=jax.Shap...  88.8 us
    pallas_call x1, Pallas kernels, gather(): pl.pallas_call(functools.partial(gather_kernel, nz, nlon, bands), out_sha...  38.5 us
    pallas_call x1, Pallas kernels, finish(): pl.pallas_call(functools.partial(finish_kernel, nlon), out_shape=jax.Shap...  13.5 us
    ppermute x1, starting transfers between devices, padded(): before = lax.ppermute(last, axis, up)  6.2 us
    slice x3, local copies, waits for them, and re-layouts, conv_features(): picked[..., column_tap:column_tap + 2 * width:2]  4.15 us
  transfers between devices with their start and end apart: 3, of which 2 were waited for; matrix products, arithmetic and copies ran while one was open for 1% of the time, Pallas kernels for 0%

profile of v1, /device:TPU:1, one launch (start us, length us, event | category | flops | bytes accessed | tf_op | source)
XLA Modules:
  0.0 170.3 jit_solution(12695680423362231255)
XLA Ops:
  0.0 0.0 copy-start.4
  0.0 1.2 copy.10
  1.2 6.2 %collective-permute-start = (bf16[73,2,128]{0,2,1:T(8,128)(2,1)S(1)}, bf16[73,2,128]{0,2,1:T(8,128)(2,1)S(1)}, u32[]{:S(2)}, u32[]{:S(2)}) collective-permute-start(bf16[73,2,128]{0,2,1:T(8,128)(2,1)S(1)} %get-tuple-element.11), channel_id=1, source_target_pairs={{0,8},{8,16},{16,24},{24,32},{32,40},{40,48},{48,56},{56,64},{64,7... | collective-permute-start | bytes 112136 | tf_op jit(solution)/shard_map/ppermute | solution.py:30
  7.4 1.9 %collective-permute-start.1 = (bf16[73,2,128]{0,2,1:T(8,128)(2,1)S(1)}, bf16[73,2,128]{0,2,1:T(8,128)(2,1)S(1)}, u32[]{:S(2)}, u32[]{:S(2)}) collective-permute-start(bf16[73,2,128]{0,2,1:T(8,128)(2,1)S(1)} %get-tuple-element.12), channel_id=1, source_target_pairs={{8,0},{16,8},{24,16},{32,24},{40,32},{48,40},{56,48},{64,56},{72,6... | collective-permute-start | bytes 112136 | tf_op jit(solution)/shard_map/ppermute | solution.py:31
  9.4 0.8 compare_and_fusion
  10.1 1.0 pad_maximum_fusion.wkv_ref
  11.1 0.1 reshape.44
  11.2 0.0 collective-permute-done
  11.2 3.3 %collective-permute-done.1 = bf16[73,2,128]{0,2,1:T(8,128)(2,1)S(1)} collective-permute-done((bf16[73,2,128]{0,2,1:T(8,128)(2,1)S(1)}, bf16[73,2,128]{0,2,1:T(8,128)(2,1)S(1)}, u32[]{:S(2)}, u32[]{:S(2)}) %collective-permute-start.1) | collective-permute-done | bytes 37408 | tf_op jit(solution)/shard_map/ppermute | solution.py:31
  14.5 1.3 collective-permute-start.2
  15.8 0.0 copy-done.4
  15.8 0.2 reshape.37
  16.0 3.2 %collective-permute-done.2 = bf16[73,12,1]{0,2,1:T(2,128)(2,1)S(1)} collective-permute-done((bf16[73,12,1]{0,2,1:T(2,128)(2,1)S(1)}, bf16[73,12,1]{0,2,1:T(2,128)(2,1)S(1)}, u32[]{:S(2)}, u32[]{:S(2)}) %collective-permute-start.2) | collective-permute-done | bytes 1784 | tf_op jit(solution)/shard_map/ppermute | solution.py:20
  19.2 0.1 maximum_maximum_fusion
  19.3 0.7 gather_fusion
  20.0 0.1 select_bitcast_fusion
  20.2 1.8 %slice.23 = bf16[73,4,5,64]{0,3,2,1:T(8,128)(2,1)S(1)} slice(bf16[73,4,5,129]{0,3,2,1:T(8,128)(2,1)S(1)} %select_bitcast_fusion), slice={[0:73:1], [0:4:1], [0:5:1], [2:129:2]} | slice | bytes 373760 | tf_op jit(solution)/shard_map/slice | solution.py:42
  22.0 1.2 slice.22
  23.2 1.2 slice.21
  24.4 0.2 maximum_bitcast_fusion
  24.6 0.9 copy.13
  25.5 1.2 reshape.36
  26.7 0.0 copy-start.3
  26.7 0.0 copy-start.1
  26.7 0.0 copy-start.2
  26.7 0.5 multiply_reduce_fusion
  27.2 0.1 multiply_convert_fusion
  27.3 0.0 copy-done.3
  27.3 38.5 %gather_features.1 = (bf16[128,64,256]{2,1,0:T(8,128)(2,1)S(1)}, bf16[8,64,256]{2,1,0:T(8,128)(2,1)S(1)}) custom-call(s32[32]{0:T(128)S(1)} %copy-done.3, bf16[4,64,256]{2,1,0:T(8,128)(2,1)S(1)} %bitcast.17), custom_call_target="tpu_custom_call" | custom-call | tf_op jit(solution)/shard_map/gather_features/pallas_call | solution.py:154
  65.8 0.0 copy-done.1
  65.8 0.0 copy-done.2
  65.8 88.8 %attend.1.o_ref = bf16[512,384]{1,0:T(8,128)(2,1)S(1)} custom-call(bf16[8192,256]{1,0:T(8,128)(2,1)S(1)} %bitcast.16, bf16[512,256]{1,0:T(8,128)(2,1)S(1)} %bitcast.18, bf16[256,256]{1,0:T(8,128)(2,1)S(1)} %copy-done.1, bf16[256,512]{1,0:T(8,128)(2,1)S(1)} %pad_maximum_fusion.wkv_ref, f32[128,128]{1,0:T(8,128)S(1)} %copy-done.2), custom_call_target="tpu_custom_call" | custom-call | tf_op jit(solution)/shard_map/attend/pallas_call | solution.py:340
  154.6 0.0 copy-start
  154.7 0.7 copy-done
  155.4 13.5 %finish.1 = bf16[64,256]{1,0:T(8,128)(2,1)} custom-call(bf16[512,384]{1,0:T(8,128)(2,1)} %copy-done, bf16[256,256]{1,0:T(8,128)(2,1)} %w_ref.1), custom_call_target="tpu_custom_call" | custom-call | tf_op jit(solution)/shard_map/finish/pallas_call | solution.py:213
  168.9 1.4 copy.15
  (5 shorter events, 0.0 us)
Async XLA Ops:
  0.0 15.8 %copy-start.4 = (bf16[5,3,73,256]{3,2,1,0:T(8,128)(2,1)S(1)}, bf16[5,3,73,256]{3,2,1,0:T(8,128)(2,1)}, u32[]{:S(2)}) copy-start(bf16[5,3,73,256]{3,2,1,0:T(8,128)(2,1)} %param.12) | copy-start | bytes 1681924
  1.2 10.0 %collective-permute-start = (bf16[73,2,128]{0,2,1:T(8,128)(2,1)S(1)}, bf16[73,2,128]{0,2,1:T(8,128)(2,1)S(1)}, u32[]{:S(2)}, u32[]{:S(2)}) collective-permute-start(bf16[73,2,128]{0,2,1:T(8,128)(2,1)S(1)} %get-tuple-element.11), channel_id=1, source_target_pairs={{0,8},{8,16},{16,24},{24,32},{32,40},{40,48},{48,56},{56,64},{64,7... | collective-permute-start | bytes 112136 | tf_op jit(solution)/shard_map/ppermute | solution.py:30
  7.4 7.1 %collective-permute-start.1 = (bf16[73,2,128]{0,2,1:T(8,128)(2,1)S(1)}, bf16[73,2,128]{0,2,1:T(8,128)(2,1)S(1)}, u32[]{:S(2)}, u32[]{:S(2)}) collective-permute-start(bf16[73,2,128]{0,2,1:T(8,128)(2,1)S(1)} %get-tuple-element.12), channel_id=1, source_target_pairs={{8,0},{16,8},{24,16},{32,24},{40,32},{48,40},{56,48},{64,56},{72,6... | collective-permute-start | bytes 112136 | tf_op jit(solution)/shard_map/ppermute | solution.py:31
  14.5 4.7 %collective-permute-start.2 = (bf16[73,12,1]{0,2,1:T(2,128)(2,1)S(1)}, bf16[73,12,1]{0,2,1:T(2,128)(2,1)S(1)}, u32[]{:S(2)}, u32[]{:S(2)}) collective-permute-start(bf16[73,12,1]{0,2,1:T(2,128)(2,1)S(1)} %pad_maximum_fusion.1), channel_id=1, source_target_pairs={{0,1},{1,2},{2,3},{3,4},{4,5},{5,6},{6,7},{7,0},{8,9},{9,10},{10,1... | collective-permute-start | bytes 5264 | tf_op jit(solution)/shard_map/ppermute | solution.py:20
  26.7 0.7 copy-start.3
  26.7 39.1 %copy-start.1 = (bf16[256,256]{1,0:T(8,128)(2,1)S(1)}, bf16[256,256]{1,0:T(8,128)(2,1)}, u32[]{:S(2)}) copy-start(bf16[256,256]{1,0:T(8,128)(2,1)} %wq_ref.1) | copy-start | bytes 393220
  26.7 39.1 %copy-start.2 = (f32[128,128]{1,0:T(8,128)S(1)}, f32[128,128]{1,0:T(8,128)}, u32[]{:S(2)}) copy-start(f32[128,128]{1,0:T(8,128)} %constant.29.clone.area_ref) | copy-start | bytes 196612
  154.6 0.7 copy-start

commit v2 on v1

v2 whole, which is shorter than its diff:
```python
import functools
import math

import jax
import jax.numpy as jnp
import numpy as np
from jax import lax
from jax.experimental import pallas as pl
from jax.experimental.pallas import tpu as pltpu
from jax.sharding import PartitionSpec as P

D = 256
H = 4
NEAR = 1
PIECES = 2


def remote(src, dst, send, recv, **where):
    return pltpu.make_async_remote_copy(
        src_ref=src, dst_ref=dst, send_sem=send, recv_sem=recv,
        device_id=where, device_id_type=pl.DeviceIdType.MESH)


def greet(peers):
    barrier = pltpu.get_barrier_semaphore()
    for peer in peers:
        pl.semaphore_signal(barrier, inc=1, device_id=peer, device_id_type=pl.DeviceIdType.MESH)
    pl.semaphore_wait(barrier, len(peers))


def ring(nz, near, n, x_ref, g_ref, sems, between):
    ys, yr, us, ur, ds, dr, cs, cr = sems
    bands = x_ref.shape[0]
    w = bands // n
    half = nz // 2
    lat = lax.axis_index("lat")
    z, yh, c = lat // 4, (lat // 2) % 2, lat % 2

    def at(zz, t, cc):
        return ((zz + nz) % nz) * 4 + (yh if t == 0 else 1 - yh) * 2 + cc

    up, down, across, twin = at(z + 1, 0, c), at(z - 1, 0, c), at(z, 1, c), at(z, 0, 1 - c)
    waits, shared, crossing = [], [], {}

    def block(i, p):
        return g_ref.at[pl.ds(i * bands + p * w, w)]

    def send(dz, t, p, sends, recvs, to):
        i = at(z + dz, t, c)
        source = x_ref.at[pl.ds(p * w, w)] if dz == 0 and t == 0 else block(i, p)
        copy = remote(source, block(i, p), sends, recvs, lat=to)
        copy.start()
        waits.append(copy)

    def arrive(dz, t, cc, p, sends, recvs, peer):
        i = at(z + dz, t, cc)
        remote(block(i, p), block(i, p), sends, recvs, lat=peer).wait_recv()

    def limits(t, p):
        return (half, nz - 1 - half) if (t + p) % 2 == 0 else (nz - 1 - half, half)

    def hop(d, p, t, s):
        if s <= limits(t, p)[d]:
            if d == 0:
                send(1 - s, t, p, us.at[p, t, s - 1], ur.at[p, t, s - 1], up)
            else:
                send(s - 1, t, p, ds.at[p, t, s - 1], dr.at[p, t, s - 1], down)

    def landed(d, p, t, s):
        if d == 0:
            arrive(-s, t, c, p, us.at[p, t, s - 1], ur.at[p, t, s - 1], down)
        else:
            arrive(s, t, c, p, ds.at[p, t, s - 1], dr.at[p, t, s - 1], up)
        hop(d, p, t, s + 1)

    def share(dz, t, p):
        k = len(shared)
        shared.append((dz, t, p))
        send(dz, t, p, cs.at[k], cr.at[k], twin)

    def cross(dz, p):
        k = len(crossing)
        crossing[dz, p] = k
        send(dz, 0, p, ys.at[k], yr.at[k], across)

    def over(s):
        for p in range(n):
            for dz in (0,) if s == 0 else (-s, s):
                k = crossing[dz, p]
                arrive(dz, 1, c, p, ys.at[k], yr.at[k], across)
                if dz == -near:
                    hop(0, p, 1, near + 1)
                if dz == near:
                    hop(1, p, 1, near + 1)
                share(dz, 1, p)

    def own(s):
        for p in range(n):
            for d in range(2):
                if s <= limits(0, p)[d]:
                    dz = s if d else -s
                    landed(d, p, 0, s)
                    if s <= near:
                        cross(dz, p)
                    share(dz, 0, p)

    def far(s):
        for p in range(n):
            for d in range(2):
                if s <= limits(1, p)[d]:
                    landed(d, p, 1, s)
                    share(s if d else -s, 1, p)

    for p in range(n):
        cross(0, p)
        hop(0, p, 0, 1)
        hop(1, p, 0, 1)
    for p in range(n):
        share(0, 0, p)
    g_ref[pl.ds(lat * bands, bands)] = x_ref[...]
    between()
    for s in range(half):
        own(s + 1)
        if s <= near:
            over(s)
        else:
            far(s)
    far(half)
    for k, (dz, t, p) in enumerate(shared):
        arrive(dz, t, 1 - c, p, cs.at[k], cr.at[k], twin)
    return waits


def encode_kernel(
    nlat, nlon, slot_ref, rows_ref, xt_ref, conv_ref, wkv_ref, area_ref,
    q_ref, kv_ref, e_ref,
    g_ref, x_ref, ext, taps, pick, hsend, hrecv, ys, yr, us, ur, ds, dr, cs, cr, qsend, qrecv,
):
    lat = lax.axis_index("lat")
    lon = lax.axis_index("lon")
    nz = nlat // 4
    high, cols, channels = xt_ref.shape
    bands, wide = x_ref.shape[0], x_ref.shape[1]
    z, yh, c = lat // 4, (lat // 2) % 2, lat % 2
    north, south = (lat + nlat - 1) % nlat, (lat + 1) % nlat
    west, east = (lon + nlon - 1) % nlon, (lon + 1) % nlon
    around = [(lon + k) % nlon for k in range(1, nlon)]
    column = z * 4 + yh * 2
    greet(
        [{"lat": p} for p in (
            ((z + 1) % nz) * 4 + yh * 2 + c,
            ((z + nz - 1) % nz) * 4 + yh * 2 + c,
            z * 4 + (1 - yh) * 2 + c,
            column + 1 - c,
            north, south,
        )]
        + [{"lon": p} for p in around]
        + [{"lat": a, "lon": b} for a in (north, south) for b in (west, east)]
    )
    strip = 16
    body, edge = pl.ds(0, cols), pl.ds(cols, strip)
    inner = pl.ds(cols - strip, strip)
    first, last = pl.ds(0, 2), pl.ds(high - 2, 2)
    below, above = pl.ds(0, 2), pl.ds(high + 2, 2)
    halo = [
        remote(xt_ref.at[last], ext.at[below, body], hsend.at[0], hrecv.at[0], lat=south),
        remote(xt_ref.at[first], ext.at[above, body], hsend.at[1], hrecv.at[1], lat=north),
        remote(xt_ref.at[:, inner], ext.at[pl.ds(2, high), edge], hsend.at[2], hrecv.at[2], lon=east),
        remote(xt_ref.at[last, inner], ext.at[below, edge], hsend.at[3], hrecv.at[3], lat=south, lon=east),
        remote(xt_ref.at[first, inner], ext.at[above, edge], hsend.at[4], hrecv.at[4], lat=north, lon=east),
    ]
    for copy in halo:
        copy.start()
    ext[2 : high + 2, 0:cols, :] = xt_ref[...]
    at_row = lax.broadcasted_iota(jnp.int32, (3 * wide, cols + strip), 0)
    at_col = lax.broadcasted_iota(jnp.int32, (3 * wide, cols + strip), 1)
    target = 2 * (at_row % wide) + at_row // wide - 1
    target = jnp.where(target < 0, cols + strip - 1, target)
    pickup = jnp.where(at_col == target, 1.0, 0.0).astype(jnp.bfloat16)
    for copy in halo:
        copy.wait_recv()
    keep_low = jnp.where(lat > 0, 1.0, 0.0)
    keep_high = jnp.where(lat < nlat - 1, 1.0, 0.0)
    for r in range(high + 4):
        tap = jnp.dot(pickup, ext[r], preferred_element_type=jnp.float32)
        if r < 2:
            tap = tap * keep_low
        if r >= high + 2:
            tap = tap * keep_high
        taps[r] = tap.astype(jnp.bfloat16)
    raw = jnp.zeros((bands * wide, D), jnp.float32)
    for k in range(rows_ref.shape[1]):
        found = [taps[2 * i + 2 + rows_ref[i, k]] for i in range(bands)]
        for t in range(3):
            part = jnp.concatenate([f[t * wide : (t + 1) * wide] for f in found], axis=0)
            raw = raw + jnp.dot(part, conv_ref[k, t], preferred_element_type=jnp.float32)
    factor = lax.rsqrt(jnp.mean(raw * raw, axis=-1, keepdims=True) + 1e-06)
    x_ref[...] = (raw * factor).astype(jnp.bfloat16).reshape(bands, wide, D)
    for copy in halo:
        copy.wait_send()

    def between():
        e_ref[...] = jnp.broadcast_to(
            area_ref[...][:, None, :], e_ref.shape
        ).astype(jnp.bfloat16)

    waits = ring(nz, NEAR, PIECES, x_ref, g_ref, (ys, yr, us, ur, ds, dr, cs, cr), between)
    chosen = g_ref[slot_ref[lat]]
    pick[...] = chosen
    q_ref[lon] = chosen
    for copy in waits:
        copy.wait_send()
    copies = []
    for k, peer in enumerate(around):
        copy = remote(pick, q_ref.at[lon], qsend.at[k], qrecv.at[k], lon=peer)
        copy.start()
        copies.append(copy)
    group = 8

    def project(i, carry):
        rows = g_ref[pl.ds(i * group, group)].reshape(group * wide, D)
        kv_ref[pl.ds(pl.multiple_of(i * group * wide, group * wide), group * wide), :] = jnp.dot(
            rows, wkv_ref[...], preferred_element_type=jnp.float32
        ).astype(jnp.bfloat16)
        return carry

    lax.fori_loop(0, g_ref.shape[0] // group, project, 0)
    for k in range(1, nlon):
        slot = (lon + nlon - k) % nlon
        remote(pick, q_ref.at[slot], qsend.at[k - 1], qrecv.at[k - 1], lon=slot).wait_recv()
    for copy in copies:
        copy.wait_send()


def encode(window_bands, support_rows, state_field, conv_weight, w_key, w_value):
    nlat, nlon = lax.axis_size("lat"), lax.axis_size("lon")
    bands = support_rows.shape[0]
    channels, high, cols = state_field.shape
    wide = cols // 2
    wkv = jnp.concatenate([w_key, w_value], axis=1)
    v = pl.BlockSpec(memory_space=pltpu.VMEM)
    s = pl.BlockSpec(memory_space=pltpu.SMEM)
    dma = pltpu.SemaphoreType.DMA
    n, nz, total = PIECES, nlat // 4, nlat * bands
    ring_sems = [dma(((2 * NEAR + 1) * n,))] * 2 + [dma((n, 2, nz // 2))] * 4 + [dma((2 * nz * n,))] * 2
    return pl.pallas_call(
        functools.partial(encode_kernel, nlat, nlon),
        out_shape=(
            jax.ShapeDtypeStruct((nlon, wide, D), jnp.bfloat16),
            jax.ShapeDtypeStruct((total * wide, 2 * D), jnp.bfloat16),
            jax.ShapeDtypeStruct((total, wide, 128), jnp.bfloat16),
        ),
        in_specs=[s, s, v, v, v, v],
        out_specs=(v, v, v),
        scratch_shapes=[
            pltpu.VMEM((total, wide, D), jnp.bfloat16),
            pltpu.VMEM((bands, wide, D), jnp.bfloat16),
            pltpu.VMEM((high + 4, cols + 16, channels), jnp.bfloat16),
            pltpu.VMEM((high + 4, 3 * wide, channels), jnp.bfloat16),
            pltpu.VMEM((wide, D), jnp.bfloat16),
            dma((5,)), dma((5,)),
        ] + ring_sems + [dma((nlon - 1,)), dma((nlon - 1,))],
        compiler_params=pltpu.CompilerParams(
            collective_id=0, has_side_effects=True, vmem_limit_bytes=30 * 1024 * 1024
        ),
        name="encode",
    )(
        window_bands, support_rows, jnp.transpose(state_field, (1, 2, 0)), conv_weight, wkv,
        jnp.asarray(area_table(total)),
    )


def finish_kernel(nlon, o_ref, w_ref, out_ref, held, send, recv):
    lon = lax.axis_index("lon")
    around = [(lon + k) % nlon for k in range(1, nlon)]
    rows = o_ref.shape[0] // nlon
    greet([{"lon": p} for p in around])
    copies = []
    for k, peer in enumerate(around):
        part = o_ref.at[pl.ds(pl.multiple_of(peer * rows, rows), rows), :]
        copy = remote(part, held.at[lon], send.at[k], recv.at[k], lon=peer)
        copy.start()
        copies.append(copy)
    held[lon] = o_ref[pl.ds(pl.multiple_of(lon * rows, rows), rows), :]
    for k in range(1, nlon):
        slot = (lon + nlon - k) % nlon
        remote(held.at[slot], held.at[slot], send.at[k - 1], recv.at[k - 1], lon=slot).wait_recv()
    logs = []
    for i in range(nlon):
        tail = held[i, :, D : D + 128].astype(jnp.float32)
        logs.append([jnp.sum(tail[:, 3 * h : 3 * h + 3], axis=1, keepdims=True) for h in range(H)])
    head = lax.broadcasted_iota(jnp.int32, (rows, D), 1) // (D // H)
    top = [functools.reduce(jnp.maximum, [logs[i][h] for i in range(nlon)]) for h in range(H)]
    share = [[jnp.exp(logs[i][h] - top[h]) for h in range(H)] for i in range(nlon)]
    total = [1.0 / sum(share[i][h] for i in range(nlon)) for h in range(H)]
    mixed = jnp.zeros((rows, D), jnp.float32)
    for i in range(nlon):
        factor = jnp.zeros((rows, D), jnp.float32)
        for h in range(H):
            factor = jnp.where(head == h, share[i][h] * total[h], factor)
        mixed = mixed + factor * held[i, :, 0:D].astype(jnp.float32)
    out_ref[...] = jnp.dot(
        mixed.astype(jnp.bfloat16), w_ref[...], preferred_element_type=jnp.float32
    ).astype(jnp.bfloat16)
    for copy in copies:
        copy.wait_send()


def finish(partial, w_out):
    nlon = lax.axis_size("lon")
    rows = partial.shape[0] // nlon
    v = pl.BlockSpec(memory_space=pltpu.VMEM)
    dma = pltpu.SemaphoreType.DMA
    return pl.pallas_call(
        functools.partial(finish_kernel, nlon),
        out_shape=jax.ShapeDtypeStruct((rows, D), jnp.bfloat16),
        in_specs=[v, v],
        out_specs=v,
        scratch_shapes=[
            pltpu.VMEM((nlon, rows, partial.shape[1]), jnp.bfloat16),
            dma((nlon - 1,)), dma((nlon - 1,)),
        ],
        compiler_params=pltpu.CompilerParams(collective_id=1, has_side_effects=True),
        name="finish",
    )(partial, w_out)


def split3(x):
    a = x.astype(jnp.bfloat16)
    r = x - a.astype(jnp.float32)
    b = r.astype(jnp.bfloat16)
    c = (r - b.astype(jnp.float32)).astype(jnp.bfloat16)
    return a, b, c

def attn_kernel(bk, qc, kv_ref, e_ref, qf_ref, wq_ref, o_ref, qa, acc, mx):
    nk = kv_ref.shape[0]
    nq = qf_ref.shape[0]
    rows = 2 * nq
    q = jnp.dot(qf_ref[...], wq_ref[...], preferred_element_type=jnp.float32).astype(jnp.bfloat16).astype(jnp.float32) * 0.125
    lane = lax.broadcasted_iota(jnp.int32, (nq, 128), 1)
    for p in range(2):
        qp = q[:, p*128:(p+1)*128]
        qa[p, 0:nq, 0:128] = jnp.where(lane < 64, qp, 0.0).astype(jnp.bfloat16)
        qa[p, nq:rows, 0:128] = jnp.where(lane >= 64, qp, 0.0).astype(jnp.bfloat16)
    elane = lax.broadcasted_iota(jnp.int32, (rows, 128), 1)
    ones = jnp.where(elane < 3, 1.0, 0.0)

    def set_shift(p, m):
        a, b, c = split3(m)
        f = lambda t: t.astype(jnp.float32)
        e = ones - jnp.where(elane == 3, f(a), 0.0) - jnp.where(elane == 4, f(b), 0.0) - jnp.where(elane == 5, f(c), 0.0)
        qa[p, :, 128:256] = e.astype(jnp.bfloat16)

    for p in range(2):
        qa[p, :, 128:256] = ones.astype(jnp.bfloat16)
    def keyed(p, kr):
        return jnp.concatenate([kv_ref[kr, p * 128 : (p + 1) * 128], e_ref[kr, :]], axis=1)

    def valued(p, kr):
        return jnp.concatenate([kv_ref[kr, D + p * 128 : D + (p + 1) * 128], e_ref[kr, :]], axis=1)

    def scores(p, qr, kr):
        return lax.dot_general(
            qa[p, qr, :], keyed(p, kr), (((1,), (1,)), ((), ())), preferred_element_type=jnp.float32
        )

    sub = pl.ds(nk//2 - 256, 512)
    nqc = rows // qc
    for p in range(2):
        for j in range(rows // 256):
            mx[p, j*256:(j+1)*256, :] = jnp.broadcast_to(jnp.max(scores(p, pl.ds(j*256, 256), sub), axis=1, keepdims=True), (256, 128))
        set_shift(p, mx[p])

    def sweep():
        acc[...] = jnp.zeros_like(acc)
        def body(i, c):
            kr = pl.ds(pl.multiple_of(i*bk, bk), bk)
            for p in range(2):
                for j in range(nqc):
                    qr = pl.ds(j*qc, qc)
                    w = jnp.exp(scores(p, qr, kr)).astype(jnp.bfloat16)
                    acc[p, qr, :] += jnp.dot(w, valued(p, kr), preferred_element_type=jnp.float32)
            return c
        lax.fori_loop(0, nk//bk, body, 0)
    sweep()
    worst = jnp.maximum(jnp.max(acc[0, :, 131:132]), jnp.max(acc[1, :, 131:132]))

    @pl.when(jnp.logical_not(worst < 1e30))
    def _():
        for p in range(2):
            qa[p, :, 128:256] = ones.astype(jnp.bfloat16)
        mx[...] = jnp.full_like(mx, -jnp.inf)
        def body(i, c):
            kr = pl.ds(pl.multiple_of(i*512, 512), 512)
            p = c
            for p in range(2):
                def qb(j, cc):
                    qr = pl.ds(pl.multiple_of(j*256, 256), 256)
                    s = jnp.max(scores(p, qr, kr), axis=1, keepdims=True)
                    mx[p, qr, :] = jnp.maximum(mx[p, qr, :], s)
                    return cc
                lax.fori_loop(0, rows//256, qb, 0)
            return c
        lax.fori_loop(0, nk//512, body, 0)
        for p in range(2):
            set_shift(p, mx[p])
        sweep()

    tail = jnp.zeros((nq, 128), jnp.float32)
    for p in range(2):
        la = acc[p, 0:nq, 131:132]; lb = acc[p, nq:rows, 131:132]
        o_ref[:, p*128:(p+1)*128] = jnp.where(lane < 64, acc[p, 0:nq, 0:128] / la, acc[p, nq:rows, 0:128] / lb).astype(jnp.bfloat16)
        for s, (l, off) in enumerate(((la, 0), (lb, nq))):
            lse = mx[p, off:off+nq, 0:1] + jnp.log(l)
            pieces = split3(lse)
            h = 2*p + s
            for t in range(3):
                tail = jnp.where(lane == 3*h + t, pieces[t].astype(jnp.float32), tail)
    o_ref[:, 256:384] = tail.astype(jnp.bfloat16)

def area_table(nlat):
    c = (np.arange(nlat, dtype=np.float64) + 0.5) * (math.pi / nlat) - math.pi/2
    a = np.log(np.cos(c)).astype(np.float32)
    t = np.zeros((nlat, 128), np.float32)
    hi = a.astype(jnp.bfloat16).astype(np.float32)
    r = a - hi; mid = r.astype(jnp.bfloat16).astype(np.float32)
    lo = (r-mid).astype(jnp.bfloat16).astype(np.float32)
    t[:,0]=hi; t[:,1]=mid; t[:,2]=lo; t[:,3:6]=1.0
    return t

def attention(kv, e, qf, wq, bk=2048, qc=256):
    nq = qf.shape[0]
    v = pl.BlockSpec(memory_space=pltpu.VMEM)
    return pl.pallas_call(
        functools.partial(attn_kernel, bk, qc),
        out_shape=jax.ShapeDtypeStruct((nq, 384), jnp.bfloat16),
        in_specs=[v] * 4,
        out_specs=v,
        scratch_shapes=[
            pltpu.VMEM((2, 2 * nq, D), jnp.bfloat16),
            pltpu.VMEM((2, 2 * nq, D), jnp.float32),
            pltpu.VMEM((2, 2 * nq, 128), jnp.float32),
        ],
        compiler_params=pltpu.CompilerParams(vmem_limit_bytes=30 * 1024 * 1024),
        name="attend",
    )(kv, e, qf, wq)


def per_device(
    state_field, support_rows, window_bands, conv_weight, w_query, w_key, w_value, w_out
):
    lat_tile = support_rows.shape[0]
    lon_tile = state_field.shape[2] // 2
    chosen, kv, e = encode(
        window_bands, support_rows, state_field, conv_weight, w_key, w_value
    )
    partial = attention(kv, e.reshape(kv.shape[0], 128), chosen.reshape(-1, D), w_query)
    return finish(partial, w_out).reshape(1, lon_tile, D)


def solution(mesh):
    return jax.shard_map(
        per_device,
        mesh=mesh,
        in_specs=(P(None, "lat", "lon"), P("lat", None), P(), P(), P(), P(), P(), P()),
        out_specs=P("lat", "lon", None),
        check_vma=False,
    )
```

time: 171 us -> 154 us (0.901)
  starting transfers between devices: 9.41 us -> 0 us
  waiting for transfers between devices: 6.5 us -> 0 us
  Pallas kernels: 141 us -> 145 us
  local copies, waits for them, and re-layouts: 10.5 us -> 7.38 us
    pallas_call x1, Pallas kernels: 38.5 us -> 48.2 us  [encode(): pl.pallas_call(functools.partial(encode_kernel, nlat, nlon), out_shape=(j...]
    ppermute x3 -> x0, starting transfers between devices: 9.41 us -> none  [the longest x1 6.2 us: padded(): before = lax.ppermute(last, axis, up)]
    ppermute x3 -> x0, waiting for transfers between devices: 6.5 us -> none  [the longest x1 3.31 us: padded(): after = lax.ppermute(leading, axis, down)]
    pallas_call x1, Pallas kernels: 88.8 us -> 84.5 us  [attention(): pl.pallas_call(functools.partial(attn_kernel, bk, qc), out_shape=jax.Shap...]
    slice x4 -> x0, local copies, waits for them, and re-layouts: 4.17 us -> none  [the longest x3 4.15 us: conv_features(): picked[..., column_tap:column_tap + 2 * width:2]]
    unnamed x12 -> x14, local copies, waits for them, and re-layouts: 3.34 us -> 7.38 us
  transfers between devices with their start and end apart: 3 -> 0, of which waited for: 2 -> 0; matrix products, arithmetic and copies ran while one was open for 1% -> 0% of each run, Pallas kernels for 0% -> 0%
where the time goes in v2:
time: 154 us; the launch traced here: 153 us
  Pallas kernels  145 us (94%)
  local copies, waits for them, and re-layouts  7.38 us (5%)
    pallas_call x1, Pallas kernels, attention(): pl.pallas_call(functools.partial(attn_kernel, bk, qc), out_shape=jax.Shap...  84.5 us
    pallas_call x1, Pallas kernels, encode(): pl.pallas_call(functools.partial(encode_kernel, nlat, nlon), out_shape=(j...  48.2 us
    pallas_call x1, Pallas kernels, finish(): pl.pallas_call(functools.partial(finish_kernel, nlon), out_shape=jax.Shap...  12 us
    unnamed x14, local copies, waits for them, and re-layouts  7.38 us

profile of v2, /device:TPU:1, one launch (start us, length us, event | category | flops | bytes accessed | tf_op | source)
XLA Modules:
  0.0 153.2 jit_solution(10360211607864067606)
XLA Ops:
  0.0 1.1 copy.10
  1.1 1.0 pad_maximum_fusion.wkv_ref
  2.1 0.0 copy-start.1
  2.1 1.1 copy-done.1
  3.2 0.0 copy-start.3
  3.2 0.8 copy-done.3
  4.0 0.0 copy-start.4
  4.0 0.7 copy-done.4
  4.7 0.0 copy-start.5
  4.7 0.7 copy-done.5
  5.4 48.2 %encode.1 = (bf16[8,64,256]{2,1,0:T(8,128)(2,1)S(1)}, bf16[8192,512]{1,0:T(8,128)(2,1)S(1)}, bf16[128,64,128]{2,1,0:T(8,128)(2,1)S(1)}) custom-call(s32[32]{0:T(128)S(1)} %copy-done.5, s32[4,5]{1,0:T(4,128)S(1)} %copy-done.4, bf16[8,128,73]{2,1,0:T(8,128)(2,1)S(1)} %bitcast.5, bf16[5,3,73,256]{3,2,1,0:T(8,128)(2,1)S(1)} %copy-done.1, ...), custom_call_target="tpu_custom_call" | custom-call | tf_op jit(solution)/shard_map/encode/pallas_call | solution.py:246
  53.6 0.0 copy-start.2
  53.6 0.9 copy-done.2
  54.5 84.5 %attend.1.o_ref = bf16[512,384]{1,0:T(8,128)(2,1)S(1)} custom-call(bf16[8192,512]{1,0:T(8,128)(2,1)S(1)} %get-tuple-element.8.kv_ref, bf16[8192,128]{1,0:T(8,128)(2,1)S(1)} %bitcast.4, bf16[512,256]{1,0:T(8,128)(2,1)S(1)} %bitcast.6, bf16[256,256]{1,0:T(8,128)(2,1)S(1)} %copy-done.2), custom_call_target="tpu_custom_call" | custom-call | tf_op jit(solution)/shard_map/attend/pallas_call | solution.py:434
  139.0 0.0 copy-start
  139.0 0.7 copy-done
  139.8 12.0 %finish.1 = bf16[64,256]{1,0:T(8,128)(2,1)} custom-call(bf16[512,384]{1,0:T(8,128)(2,1)} %copy-done, bf16[256,256]{1,0:T(8,128)(2,1)} %w_ref.1), custom_call_target="tpu_custom_call" | custom-call | tf_op jit(solution)/shard_map/finish/pallas_call | solution.py:314
  151.8 1.4 copy.12
Async XLA Ops:
  2.1 1.1 copy-start.1
  3.2 0.8 copy-start.3
  4.0 0.7 copy-start.4
  4.7 0.7 copy-start.5
  53.6 0.9 copy-start.2
  139.0 0.8 copy-start

commit v3 on v2

v3 whole, which is shorter than its diff:
```python
import functools
import math

import jax
import jax.numpy as jnp
import numpy as np
from jax import lax
from jax.experimental import pallas as pl
from jax.experimental.pallas import tpu as pltpu
from jax.sharding import PartitionSpec as P

D = 256
H = 4
NEAR = 1
PIECES = 2
BLOCK_KEYS = 2048


def remote(src, dst, send, recv, **where):
    return pltpu.make_async_remote_copy(
        src_ref=src, dst_ref=dst, send_sem=send, recv_sem=recv,
        device_id=where, device_id_type=pl.DeviceIdType.MESH)


def greet(peers):
    barrier = pltpu.get_barrier_semaphore()
    for peer in peers:
        pl.semaphore_signal(barrier, inc=1, device_id=peer, device_id_type=pl.DeviceIdType.MESH)
    pl.semaphore_wait(barrier, len(peers))


def ring(nz, near, n, x_ref, g_ref, sems, between):
    ys, yr, us, ur, ds, dr, cs, cr = sems
    bands = x_ref.shape[0]
    w = bands // n
    half = nz // 2
    lat = lax.axis_index("lat")
    z, yh, c = lat // 4, (lat // 2) % 2, lat % 2

    def at(zz, t, cc):
        return ((zz + nz) % nz) * 4 + (yh if t == 0 else 1 - yh) * 2 + cc

    up, down, across, twin = at(z + 1, 0, c), at(z - 1, 0, c), at(z, 1, c), at(z, 0, 1 - c)
    waits, shared, crossing = [], [], {}

    def block(i, p):
        return g_ref.at[pl.ds(i * bands + p * w, w)]

    def send(dz, t, p, sends, recvs, to):
        i = at(z + dz, t, c)
        source = x_ref.at[pl.ds(p * w, w)] if dz == 0 and t == 0 else block(i, p)
        copy = remote(source, block(i, p), sends, recvs, lat=to)
        copy.start()
        waits.append(copy)

    def arrive(dz, t, cc, p, sends, recvs, peer):
        i = at(z + dz, t, cc)
        remote(block(i, p), block(i, p), sends, recvs, lat=peer).wait_recv()

    def limits(t, p):
        return (half, nz - 1 - half) if (t + p) % 2 == 0 else (nz - 1 - half, half)

    def hop(d, p, t, s):
        if s <= limits(t, p)[d]:
            if d == 0:
                send(1 - s, t, p, us.at[p, t, s - 1], ur.at[p, t, s - 1], up)
            else:
                send(s - 1, t, p, ds.at[p, t, s - 1], dr.at[p, t, s - 1], down)

    def landed(d, p, t, s):
        if d == 0:
            arrive(-s, t, c, p, us.at[p, t, s - 1], ur.at[p, t, s - 1], down)
        else:
            arrive(s, t, c, p, ds.at[p, t, s - 1], dr.at[p, t, s - 1], up)
        hop(d, p, t, s + 1)

    def share(dz, t, p):
        k = len(shared)
        shared.append((dz, t, p))
        send(dz, t, p, cs.at[k], cr.at[k], twin)

    def cross(dz, p):
        k = len(crossing)
        crossing[dz, p] = k
        send(dz, 0, p, ys.at[k], yr.at[k], across)

    def over(s):
        for p in range(n):
            for dz in (0,) if s == 0 else (-s, s):
                k = crossing[dz, p]
                arrive(dz, 1, c, p, ys.at[k], yr.at[k], across)
                if dz == -near:
                    hop(0, p, 1, near + 1)
                if dz == near:
                    hop(1, p, 1, near + 1)
                share(dz, 1, p)

    def own(s):
        for p in range(n):
            for d in range(2):
                if s <= limits(0, p)[d]:
                    dz = s if d else -s
                    landed(d, p, 0, s)
                    if s <= near:
                        cross(dz, p)
                    share(dz, 0, p)

    def far(s):
        for p in range(n):
            for d in range(2):
                if s <= limits(1, p)[d]:
                    landed(d, p, 1, s)
                    share(s if d else -s, 1, p)

    for p in range(n):
        cross(0, p)
        hop(0, p, 0, 1)
        hop(1, p, 0, 1)
    for p in range(n):
        share(0, 0, p)
    g_ref[pl.ds(lat * bands, bands)] = x_ref[...]
    between()
    for s in range(half):
        own(s + 1)
        if s <= near:
            over(s)
        else:
            far(s)
    far(half)
    for k, (dz, t, p) in enumerate(shared):
        arrive(dz, t, 1 - c, p, cs.at[k], cr.at[k], twin)
    return waits


def whole_kernel(
    nlat, nlon, block_keys, slot_ref, rows_ref, xt_ref, conv_in, wq_in, wk_in, wv_in, wo_in, area_in, out_ref,
    conv_ref, wq_ref, wk_ref, wv_ref, wo_ref, area_ref, load,
    g_ref, x_ref, ext, taps, pick, q_ref, kv_ref, e_ref, qa, stage, held,
    hsend, hrecv, ys, yr, us, ur, ds, dr, cs, cr, qsend, qrecv, osend, orecv,
):
    loads = [
        pltpu.make_async_copy(source, target, load.at[i])
        for i, (source, target) in enumerate((
            (conv_in, conv_ref), (area_in, area_ref), (wk_in, wk_ref),
            (wv_in, wv_ref), (wq_in, wq_ref), (wo_in, wo_ref),
        ))
    ]
    for copy in loads:
        copy.start()
    lat = lax.axis_index("lat")
    lon = lax.axis_index("lon")
    nz = nlat // 4
    high, cols, channels = xt_ref.shape
    bands, wide = x_ref.shape[0], x_ref.shape[1]
    z, yh, c = lat // 4, (lat // 2) % 2, lat % 2
    north, south = (lat + nlat - 1) % nlat, (lat + 1) % nlat
    west, east = (lon + nlon - 1) % nlon, (lon + 1) % nlon
    around = [(lon + k) % nlon for k in range(1, nlon)]
    column = z * 4 + yh * 2
    greet(
        [{"lat": p} for p in (
            ((z + 1) % nz) * 4 + yh * 2 + c,
            ((z + nz - 1) % nz) * 4 + yh * 2 + c,
            z * 4 + (1 - yh) * 2 + c,
            column + 1 - c,
            north, south,
        )]
        + [{"lon": p} for p in around]
        + [{"lat": a, "lon": b} for a in (north, south) for b in (west, east)]
    )
    strip = 16
    body, edge = pl.ds(0, cols), pl.ds(cols, strip)
    inner = pl.ds(cols - strip, strip)
    first, last = pl.ds(0, 2), pl.ds(high - 2, 2)
    below, above = pl.ds(0, 2), pl.ds(high + 2, 2)
    halo = [
        remote(xt_ref.at[last], ext.at[below, body], hsend.at[0], hrecv.at[0], lat=south),
        remote(xt_ref.at[first], ext.at[above, body], hsend.at[1], hrecv.at[1], lat=north),
        remote(xt_ref.at[:, inner], ext.at[pl.ds(2, high), edge], hsend.at[2], hrecv.at[2], lon=east),
        remote(xt_ref.at[last, inner], ext.at[below, edge], hsend.at[3], hrecv.at[3], lat=south, lon=east),
        remote(xt_ref.at[first, inner], ext.at[above, edge], hsend.at[4], hrecv.at[4], lat=north, lon=east),
    ]
    for copy in halo:
        copy.start()
    ext[2 : high + 2, 0:cols, :] = xt_ref[...]
    at_row = lax.broadcasted_iota(jnp.int32, (3 * wide, cols + strip), 0)
    at_col = lax.broadcasted_iota(jnp.int32, (3 * wide, cols + strip), 1)
    target = 2 * (at_row % wide) + at_row // wide - 1
    target = jnp.where(target < 0, cols + strip - 1, target)
    pickup = jnp.where(at_col == target, 1.0, 0.0).astype(jnp.bfloat16)
    for copy in halo:
        copy.wait_recv()
    keep_low = jnp.where(lat > 0, 1.0, 0.0)
    keep_high = jnp.where(lat < nlat - 1, 1.0, 0.0)
    for r in range(high + 4):
        tap = jnp.dot(pickup, ext[r], preferred_element_type=jnp.float32)
        if r < 2:
            tap = tap * keep_low
        if r >= high + 2:
            tap = tap * keep_high
        taps[r] = tap.astype(jnp.bfloat16)
    loads[0].wait()
    raw = jnp.zeros((bands * wide, D), jnp.float32)
    for k in range(rows_ref.shape[1]):
        found = [taps[2 * i + 2 + rows_ref[i, k]] for i in range(bands)]
        for t in range(3):
            part = jnp.concatenate([f[t * wide : (t + 1) * wide] for f in found], axis=0)
            raw = raw + jnp.dot(part, conv_ref[k, t], preferred_element_type=jnp.float32)
    factor = lax.rsqrt(jnp.mean(raw * raw, axis=-1, keepdims=True) + 1e-06)
    x_ref[...] = (raw * factor).astype(jnp.bfloat16).reshape(bands, wide, D)
    for copy in halo:
        copy.wait_send()

    def between():
        for copy in loads[1:]:
            copy.wait()
        e_ref[...] = jnp.broadcast_to(
            area_ref[...][:, None, :], (nlat * bands, wide, 128)
        ).reshape(e_ref.shape).astype(jnp.bfloat16)

    waits = ring(nz, NEAR, PIECES, x_ref, g_ref, (ys, yr, us, ur, ds, dr, cs, cr), between)
    chosen = g_ref[slot_ref[lat]]
    pick[...] = chosen
    q_ref[lon] = chosen
    for copy in waits:
        copy.wait_send()
    copies = []
    for k, peer in enumerate(around):
        copy = remote(pick, q_ref.at[lon], qsend.at[k], qrecv.at[k], lon=peer)
        copy.start()
        copies.append(copy)
    group = 8

    def project(i, carry):
        rows = g_ref[pl.ds(i * group, group)].reshape(group * wide, D)
        for j, w_ref in enumerate((wk_ref, wv_ref)):
            kv_ref[pl.ds(pl.multiple_of(i * group * wide, group * wide), group * wide), j * D : (j + 1) * D] = (
                jnp.dot(rows, w_ref[...], preferred_element_type=jnp.float32).astype(jnp.bfloat16)
            )
        return carry

    lax.fori_loop(0, g_ref.shape[0] // group, project, 0)

    outgoing = []
    for first_step in range(1, nlon + 1, 2):
        pair = (first_step, first_step + 1)
        for step in pair:
            if step < nlon:
                slot = (lon + step) % nlon
                k = nlon - step
                remote(pick, q_ref.at[slot], qsend.at[k - 1], qrecv.at[k - 1], lon=slot).wait_recv()
        mine = attend(
            jnp.concatenate([q_ref[(lon + step) % nlon] for step in pair], axis=0),
            wq_ref, kv_ref, e_ref, qa, block_keys,
        )
        for i, step in enumerate(pair):
            part = mine[i * wide : (i + 1) * wide]
            if step < nlon:
                stage[step - 1] = part
                peer = (lon + step) % nlon
                copy = remote(stage.at[step - 1], held.at[lon], osend.at[step - 1], orecv.at[step - 1], lon=peer)
                copy.start()
                outgoing.append(copy)
            else:
                held[lon] = part
    for k in range(1, nlon):
        slot = (lon + nlon - k) % nlon
        remote(stage.at[k - 1], held.at[slot], osend.at[k - 1], orecv.at[k - 1], lon=slot).wait_recv()
    out_ref[...] = merge(held, wo_ref, nlon)
    for copy in copies + outgoing:
        copy.wait_send()


def attend(features, wq_ref, kv_ref, e_ref, qa, block_keys):
    count = features.shape[0]
    rows = 2 * count
    q = jnp.dot(features, wq_ref[...], preferred_element_type=jnp.float32)
    q = q.astype(jnp.bfloat16).astype(jnp.float32) * (1.0 / math.sqrt(D // H))
    lane = lax.broadcasted_iota(jnp.int32, (count, 128), 1)
    marks = jnp.where(lax.broadcasted_iota(jnp.int32, (rows, 128), 1) < 3, 1.0, 0.0)
    tall = lax.broadcasted_iota(jnp.int32, (count, 128), 1)
    tail = jnp.zeros((count, 128), jnp.float32)
    for p in range(2):
        qp = q[:, p * 128 : (p + 1) * 128]
        qa[p, 0:count, 0:128] = jnp.where(lane < 64, qp, 0.0).astype(jnp.bfloat16)
        qa[p, count:rows, 0:128] = jnp.where(lane >= 64, qp, 0.0).astype(jnp.bfloat16)
        qa[p, :, 128:256] = marks.astype(jnp.bfloat16)
    top = [jnp.full((rows, 1), -1e30, jnp.float32)] * 2
    total = [jnp.zeros((rows, D), jnp.float32)] * 2
    for i in range(kv_ref.shape[0] // block_keys):
        keys = pl.ds(i * block_keys, block_keys)
        extra = e_ref[keys, :]
        for p in range(2):
            keyed = jnp.concatenate([kv_ref[keys, p * 128 : (p + 1) * 128], extra], axis=1)
            valued = jnp.concatenate([kv_ref[keys, D + p * 128 : D + (p + 1) * 128], extra], axis=1)
            s = lax.dot_general(
                qa[p], keyed, (((1,), (1,)), ((), ())), preferred_element_type=jnp.float32
            )
            best = jnp.maximum(top[p], jnp.max(s, axis=1, keepdims=True))
            w = jnp.exp(s - best).astype(jnp.bfloat16)
            update = jnp.dot(w, valued, preferred_element_type=jnp.float32)
            total[p] = update if i == 0 else total[p] * jnp.exp(top[p] - best) + update
            top[p] = best
    mixed = []
    for p in range(2):
        sums = total[p][:, 131:132]
        scaled = total[p][:, 0:128] / sums
        logs = top[p] + jnp.log(sums)
        mixed.append(jnp.where(lane < 64, scaled[0:count], scaled[count:rows]))
        for side in range(2):
            for t, piece in enumerate(split3(logs[side * count : (side + 1) * count])):
                tail = jnp.where(tall == 3 * (2 * p + side) + t, piece.astype(jnp.float32), tail)
    return jnp.concatenate(mixed + [tail], axis=1).astype(jnp.bfloat16)


def merge(held, w_ref, nlon):
    rows = held.shape[1]
    logs = []
    for i in range(nlon):
        tail = held[i, :, D : D + 128].astype(jnp.float32)
        logs.append([jnp.sum(tail[:, 3 * h : 3 * h + 3], axis=1, keepdims=True) for h in range(H)])
    head = lax.broadcasted_iota(jnp.int32, (rows, D), 1) // (D // H)
    top = [functools.reduce(jnp.maximum, [logs[i][h] for i in range(nlon)]) for h in range(H)]
    share = [[jnp.exp(logs[i][h] - top[h]) for h in range(H)] for i in range(nlon)]
    total = [1.0 / sum(share[i][h] for i in range(nlon)) for h in range(H)]
    mixed = jnp.zeros((rows, D), jnp.float32)
    for i in range(nlon):
        factor = jnp.zeros((rows, D), jnp.float32)
        for h in range(H):
            factor = jnp.where(head == h, share[i][h] * total[h], factor)
        mixed = mixed + factor * held[i, :, 0:D].astype(jnp.float32)
    return jnp.dot(
        mixed.astype(jnp.bfloat16), w_ref[...], preferred_element_type=jnp.float32
    ).astype(jnp.bfloat16)


def whole(window_bands, support_rows, state_field, conv_weight, w_query, w_key, w_value, w_out):
    nlat, nlon = lax.axis_size("lat"), lax.axis_size("lon")
    bands = support_rows.shape[0]
    channels, high, cols = state_field.shape
    wide = cols // 2
    v = pl.BlockSpec(memory_space=pltpu.VMEM)
    s = pl.BlockSpec(memory_space=pltpu.SMEM)
    far = pl.BlockSpec(memory_space=pl.ANY)
    dma = pltpu.SemaphoreType.DMA
    half = jnp.bfloat16
    n, nz, total = PIECES, nlat // 4, nlat * bands
    ring_sems = [dma(((2 * NEAR + 1) * n,))] * 2 + [dma((n, 2, nz // 2))] * 4 + [dma((2 * nz * n,))] * 2
    return pl.pallas_call(
        functools.partial(whole_kernel, nlat, nlon, BLOCK_KEYS),
        out_shape=jax.ShapeDtypeStruct((wide, D), half),
        in_specs=[s, s, v] + [far] * 6,
        out_specs=v,
        scratch_shapes=[
            pltpu.VMEM(conv_weight.shape, half),
            pltpu.VMEM((D, D), half), pltpu.VMEM((D, D), half),
            pltpu.VMEM((D, D), half), pltpu.VMEM((D, D), half),
            pltpu.VMEM((total, 128), jnp.float32),
            dma((6,)),
            pltpu.VMEM((total, wide, D), half),
            pltpu.VMEM((bands, wide, D), half),
            pltpu.VMEM((high + 4, cols + 16, channels), half),
            pltpu.VMEM((high + 4, 3 * wide, channels), half),
            pltpu.VMEM((wide, D), half),
            pltpu.VMEM((nlon, wide, D), half),
            pltpu.VMEM((total * wide, 2 * D), half),
            pltpu.VMEM((total * wide, 128), half),
            pltpu.VMEM((2, 4 * wide, D), half),
            pltpu.VMEM((nlon - 1, wide, D + 128), half),
            pltpu.VMEM((nlon, wide, D + 128), half),
            dma((5,)), dma((5,)),
        ] + ring_sems + [dma((nlon - 1,))] * 4,
        compiler_params=pltpu.CompilerParams(
            collective_id=0, has_side_effects=True, vmem_limit_bytes=60 * 1024 * 1024
        ),
        name="whole",
    )(
        window_bands, support_rows, jnp.transpose(state_field, (1, 2, 0)), conv_weight,
        w_query, w_key, w_value, w_out, jnp.asarray(area_table(total)),
    )


def split3(x):
    a = x.astype(jnp.bfloat16)
    r = x - a.astype(jnp.float32)
    b = r.astype(jnp.bfloat16)
    c = (r - b.astype(jnp.float32)).astype(jnp.bfloat16)
    return a, b, c

def area_table(nlat):
    c = (np.arange(nlat, dtype=np.float64) + 0.5) * (math.pi / nlat) - math.pi/2
    a = np.log(np.cos(c)).astype(np.float32)
    t = np.zeros((nlat, 128), np.float32)
    hi = a.astype(jnp.bfloat16).astype(np.float32)
    r = a - hi; mid = r.astype(jnp.bfloat16).astype(np.float32)
    lo = (r-mid).astype(jnp.bfloat16).astype(np.float32)
    t[:,0]=hi; t[:,1]=mid; t[:,2]=lo; t[:,3:6]=1.0
    return t

def per_device(
    state_field, support_rows, window_bands, conv_weight, w_query, w_key, w_value, w_out
):
    lon_tile = state_field.shape[2] // 2
    result = whole(
        window_bands, support_rows, state_field, conv_weight, w_query, w_key, w_value, w_out
    )
    return result.reshape(1, lon_tile, D)


def solution(mesh):
    return jax.shard_map(
        per_device,
        mesh=mesh,
        in_specs=(P(None, "lat", "lon"), P("lat", None), P(), P(), P(), P(), P(), P()),
        out_specs=P("lat", "lon", None),
        check_vma=False,
    )
```

time: 154 us -> 81.1 us (0.53)
  Pallas kernels: 145 us -> 77.8 us
  local copies, waits for them, and re-layouts: 7.38 us -> 3.16 us
    pallas_call x3 -> x1, Pallas kernels: 145 us -> 77.8 us  [whole(): pl.pallas_call(functools.partial(whole_kernel, nlat, nlon, BLOCK_KEYS), o...]
    unnamed x14 -> x2, local copies, waits for them, and re-layouts: 7.38 us -> 3.16 us
where the time goes in v3:
time: 81.1 us; the launch traced here: 80.9 us
  Pallas kernels  77.8 us (96%)
  local copies, waits for them, and re-layouts  3.16 us (4%)
    pallas_call x1, Pallas kernels, whole(): pl.pallas_call(functools.partial(whole_kernel, nlat, nlon, BLOCK_KEYS), o...  77.8 us
    unnamed x2, local copies, waits for them, and re-layouts  3.16 us

profile of v3, /device:TPU:1, one launch (start us, length us, event | category | flops | bytes accessed | tf_op | source)
XLA Modules:
  0.0 80.9 jit_solution(3068502941344454612)
XLA Ops:
  0.0 1.8 %copy.10 = bf16[73,8,128]{0,2,1:T(8,128)(2,1)} copy(bf16[73,8,128]{2,1,0:T(8,128)(2,1)} %param.9) | data formatting | bytes 299008 | tf_op args[0]
  1.8 77.8 %whole.1 = bf16[64,256]{1,0:T(8,128)(2,1)} custom-call(s32[32]{0:T(128)} %slot_ref.1, s32[4,5]{1,0:T(4,128)} %rows_ref.1, bf16[8,128,73]{2,1,0:T(8,128)(2,1)} %bitcast.2, bf16[5,3,73,256]{3,2,1,0:T(8,128)(2,1)} %conv_in.1, bf16[256,256]{1,0:T(8,128)(2,1)} %wq_in.1, bf16[256,256]{1,0:T(8,128)(2,1)} %wk_in.1, bf16[256,256]{1,0:T(8,128)(2,1)} %wv_in.1, ...), custom_call_target="tpu_custom_call" | custom-call | tf_op jit(solution)/shard_map/whole/pallas_call | solution.py:349
  79.5 1.4 %copy.12 = bf16[1,64,256]{2,1,0:T(8,128)(2,1)} copy(bf16[1,64,256]{2,1,0:T(8,128)(2,1)} %bitcast.3) | data formatting | bytes 65536

commit v4 on v3

--- a/solution.py
+++ b/solution.py
@@ -133,7 +133,7 @@
 
 
 def whole_kernel(
-    nlat, nlon, block_keys, slot_ref, rows_ref, xt_ref, conv_in, wq_in, wk_in, wv_in, wo_in, area_in, out_ref,
+    nlat, nlon, block_keys, slot_ref, rows_ref, xt_in, conv_in, wq_in, wk_in, wv_in, wo_in, area_in, out_ref,
     conv_ref, wq_ref, wk_ref, wv_ref, wo_ref, area_ref, load,
     g_ref, x_ref, ext, taps, pick, q_ref, kv_ref, e_ref, qa, stage, held,
     hsend, hrecv, ys, yr, us, ur, ds, dr, cs, cr, qsend, qrecv, osend, orecv,
@@ -150,7 +150,9 @@
     lat = lax.axis_index("lat")
     lon = lax.axis_index("lon")
     nz = nlat // 4
-    high, cols, channels = xt_ref.shape
+    high, cols, channels = xt_in.shape
+    state = pltpu.make_async_copy(xt_in, ext.at[pl.ds(2, high), pl.ds(0, cols)], load.at[6])
+    state.start()
     bands, wide = x_ref.shape[0], x_ref.shape[1]
     z, yh, c = lat // 4, (lat // 2) % 2, lat % 2
     north, south = (lat + nlat - 1) % nlat, (lat + 1) % nlat
@@ -174,31 +176,36 @@
     first, last = pl.ds(0, 2), pl.ds(high - 2, 2)
     below, above = pl.ds(0, 2), pl.ds(high + 2, 2)
     halo = [
-        remote(xt_ref.at[last], ext.at[below, body], hsend.at[0], hrecv.at[0], lat=south),
-        remote(xt_ref.at[first], ext.at[above, body], hsend.at[1], hrecv.at[1], lat=north),
-        remote(xt_ref.at[:, inner], ext.at[pl.ds(2, high), edge], hsend.at[2], hrecv.at[2], lon=east),
-        remote(xt_ref.at[last, inner], ext.at[below, edge], hsend.at[3], hrecv.at[3], lat=south, lon=east),
-        remote(xt_ref.at[first, inner], ext.at[above, edge], hsend.at[4], hrecv.at[4], lat=north, lon=east),
+        remote(xt_in.at[last], ext.at[below, body], hsend.at[0], hrecv.at[0], lat=south),
+        remote(xt_in.at[first], ext.at[above, body], hsend.at[1], hrecv.at[1], lat=north),
+        remote(xt_in.at[:, inner], ext.at[pl.ds(2, high), edge], hsend.at[2], hrecv.at[2], lon=east),
+        remote(xt_in.at[last, inner], ext.at[below, edge], hsend.at[3], hrecv.at[3], lat=south, lon=east),
+        remote(xt_in.at[first, inner], ext.at[above, edge], hsend.at[4], hrecv.at[4], lat=north, lon=east),
     ]
     for copy in halo:
         copy.start()
-    ext[2 : high + 2, 0:cols, :] = xt_ref[...]
-    at_row = lax.broadcasted_iota(jnp.int32, (3 * wide, cols + strip), 0)
-    at_col = lax.broadcasted_iota(jnp.int32, (3 * wide, cols + strip), 1)
+    at_row = lax.broadcasted_iota(jnp.int32, (3 * wide, cols), 0)
+    at_col = lax.broadcasted_iota(jnp.int32, (3 * wide, cols), 1)
     target = 2 * (at_row % wide) + at_row // wide - 1
-    target = jnp.where(target < 0, cols + strip - 1, target)
     pickup = jnp.where(at_col == target, 1.0, 0.0).astype(jnp.bfloat16)
+    state.wait()
+
+    def tapped(r):
+        return jnp.dot(pickup, ext[r, 0:cols, :], preferred_element_type=jnp.float32)
+
+    for r in range(2, high + 2):
+        taps[r] = tapped(r).astype(jnp.bfloat16)
     for copy in halo:
         copy.wait_recv()
     keep_low = jnp.where(lat > 0, 1.0, 0.0)
     keep_high = jnp.where(lat < nlat - 1, 1.0, 0.0)
     for r in range(high + 4):
-        tap = jnp.dot(pickup, ext[r], preferred_element_type=jnp.float32)
-        if r < 2:
-            tap = tap * keep_low
-        if r >= high + 2:
-            tap = tap * keep_high
-        taps[r] = tap.astype(jnp.bfloat16)
+        brink = ext[r, cols + strip - 1 : cols + strip, :].astype(jnp.float32)
+        if r < 2 or r >= high + 2:
+            keep = keep_low if r < 2 else keep_high
+            taps[r] = (tapped(r) * keep).astype(jnp.bfloat16)
+            brink = brink * keep
+        taps[r, 0:1, :] = brink.astype(jnp.bfloat16)
     loads[0].wait()
     raw = jnp.zeros((bands * wide, D), jnp.float32)
     for k in range(rows_ref.shape[1]):
@@ -222,9 +229,7 @@
     chosen = g_ref[slot_ref[lat]]
     pick[...] = chosen
     q_ref[lon] = chosen
-    for copy in waits:
-        copy.wait_send()
-    copies = []
+    copies = list(waits)
     for k, peer in enumerate(around):
         copy = remote(pick, q_ref.at[lon], qsend.at[k], qrecv.at[k], lon=peer)
         copy.start()
@@ -242,10 +247,10 @@
     lax.fori_loop(0, g_ref.shape[0] // group, project, 0)
 
     outgoing = []
-    for first_step in range(1, nlon + 1, 2):
+    for first_step in range(0, nlon, 2):
         pair = (first_step, first_step + 1)
         for step in pair:
-            if step < nlon:
+            if step > 0:
                 slot = (lon + step) % nlon
                 k = nlon - step
                 remote(pick, q_ref.at[slot], qsend.at[k - 1], qrecv.at[k - 1], lon=slot).wait_recv()
@@ -255,7 +260,7 @@
         )
         for i, step in enumerate(pair):
             part = mine[i * wide : (i + 1) * wide]
-            if step < nlon:
+            if step > 0:
                 stage[step - 1] = part
                 peer = (lon + step) % nlon
                 copy = remote(stage.at[step - 1], held.at[lon], osend.at[step - 1], orecv.at[step - 1], lon=peer)
@@ -349,14 +354,14 @@
     return pl.pallas_call(
         functools.partial(whole_kernel, nlat, nlon, BLOCK_KEYS),
         out_shape=jax.ShapeDtypeStruct((wide, D), half),
-        in_specs=[s, s, v] + [far] * 6,
+        in_specs=[s, s] + [far] * 7,
         out_specs=v,
         scratch_shapes=[
             pltpu.VMEM(conv_weight.shape, half),
             pltpu.VMEM((D, D), half), pltpu.VMEM((D, D), half),
             pltpu.VMEM((D, D), half), pltpu.VMEM((D, D), half),
             pltpu.VMEM((total, 128), jnp.float32),
-            dma((6,)),
+            dma((7,)),
             pltpu.VMEM((total, wide, D), half),
             pltpu.VMEM((bands, wide, D), half),
             pltpu.VMEM((high + 4, cols + 16, channels), half),

time: 81.1 us -> 80.9 us (level)
  no operation moved by 1% of the time
where the time goes in v4:
time: 80.9 us; the launch traced here: 80.7 us
  Pallas kernels  77.6 us (96%)
  local copies, waits for them, and re-layouts  3.16 us (4%)
    pallas_call x1, Pallas kernels, whole(): pl.pallas_call(functools.partial(whole_kernel, nlat, nlon, BLOCK_KEYS), o...  77.6 us
    unnamed x2, local copies, waits for them, and re-layouts  3.16 us

profile of v4, /device:TPU:1, one launch (start us, length us, event | category | flops | bytes accessed | tf_op | source)
XLA Modules:
  0.0 80.7 jit_solution(6654821842348847312)
XLA Ops:
  0.0 1.8 %copy.10 = bf16[73,8,128]{0,2,1:T(8,128)(2,1)} copy(bf16[73,8,128]{2,1,0:T(8,128)(2,1)} %param.9) | data formatting | bytes 299008 | tf_op args[0]
  1.8 77.6 %whole.1 = bf16[64,256]{1,0:T(8,128)(2,1)} custom-call(s32[32]{0:T(128)} %slot_ref.1, s32[4,5]{1,0:T(4,128)} %rows_ref.1, bf16[8,128,73]{2,1,0:T(8,128)(2,1)} %bitcast.2, bf16[5,3,73,256]{3,2,1,0:T(8,128)(2,1)} %conv_in.1, bf16[256,256]{1,0:T(8,128)(2,1)} %wq_in.1, bf16[256,256]{1,0:T(8,128)(2,1)} %wk_in.1, bf16[256,256]{1,0:T(8,128)(2,1)} %wv_in.1, ...), custom_call_target="tpu_custom_call" | custom-call | tf_op jit(solution)/shard_map/whole/pallas_call | solution.py:354
  79.3 1.4 %copy.12 = bf16[1,64,256]{2,1,0:T(8,128)(2,1)} copy(bf16[1,64,256]{2,1,0:T(8,128)(2,1)} %bitcast.3) | data formatting | bytes 65536

commit v5 on v4

--- a/solution.py
+++ b/solution.py
@@ -133,8 +133,8 @@
 
 
 def whole_kernel(
-    nlat, nlon, block_keys, slot_ref, rows_ref, xt_in, conv_in, wq_in, wk_in, wv_in, wo_in, area_in, out_ref,
-    conv_ref, wq_ref, wk_ref, wv_ref, wo_ref, area_ref, load,
+    nlat, nlon, block_keys, slot_ref, rows_ref, xt_in, conv_in, wq_in, wk_in, wv_in, area_in, out_ref,
+    conv_ref, wq_ref, wk_ref, wv_ref, area_ref, load,
     g_ref, x_ref, ext, taps, pick, q_ref, kv_ref, e_ref, qa, stage, held,
     hsend, hrecv, ys, yr, us, ur, ds, dr, cs, cr, qsend, qrecv, osend, orecv,
 ):
@@ -142,7 +142,7 @@
         pltpu.make_async_copy(source, target, load.at[i])
         for i, (source, target) in enumerate((
             (conv_in, conv_ref), (area_in, area_ref), (wk_in, wk_ref),
-            (wv_in, wv_ref), (wq_in, wq_ref), (wo_in, wo_ref),
+            (wv_in, wv_ref), (wq_in, wq_ref),
         ))
     ]
     for copy in loads:
@@ -151,7 +151,7 @@
     lon = lax.axis_index("lon")
     nz = nlat // 4
     high, cols, channels = xt_in.shape
-    state = pltpu.make_async_copy(xt_in, ext.at[pl.ds(2, high), pl.ds(0, cols)], load.at[6])
+    state = pltpu.make_async_copy(xt_in, ext.at[pl.ds(2, high), pl.ds(0, cols)], load.at[5])
     state.start()
     bands, wide = x_ref.shape[0], x_ref.shape[1]
     z, yh, c = lat // 4, (lat // 2) % 2, lat % 2
@@ -247,8 +247,8 @@
     lax.fori_loop(0, g_ref.shape[0] // group, project, 0)
 
     outgoing = []
-    for first_step in range(0, nlon, 2):
-        pair = (first_step, first_step + 1)
+    for first_step in range(1, nlon, 2):
+        pair = (first_step, (first_step + 1) % nlon)
         for step in pair:
             if step > 0:
                 slot = (lon + step) % nlon
@@ -268,10 +268,13 @@
                 outgoing.append(copy)
             else:
                 held[lon] = part
-    for k in range(1, nlon):
+    def ready(k):
         slot = (lon + nlon - k) % nlon
-        remote(stage.at[k - 1], held.at[slot], osend.at[k - 1], orecv.at[k - 1], lon=slot).wait_recv()
-    out_ref[...] = merge(held, wo_ref, nlon)
+        if k > 0:
+            remote(stage.at[k - 1], held.at[slot], osend.at[k - 1], orecv.at[k - 1], lon=slot).wait_recv()
+        return slot
+
+    out_ref[...] = merge(held, ready, nlon)
     for copy in copies + outgoing:
         copy.wait_send()
 
@@ -318,12 +321,14 @@
     return jnp.concatenate(mixed + [tail], axis=1).astype(jnp.bfloat16)
 
 
-def merge(held, w_ref, nlon):
+def merge(held, ready, nlon):
     rows = held.shape[1]
-    logs = []
+    logs, parts = [], []
     for i in range(nlon):
-        tail = held[i, :, D : D + 128].astype(jnp.float32)
+        slot = ready(i)
+        tail = held[slot, :, D : D + 128].astype(jnp.float32)
         logs.append([jnp.sum(tail[:, 3 * h : 3 * h + 3], axis=1, keepdims=True) for h in range(H)])
+        parts.append(slot)
     head = lax.broadcasted_iota(jnp.int32, (rows, D), 1) // (D // H)
     top = [functools.reduce(jnp.maximum, [logs[i][h] for i in range(nlon)]) for h in range(H)]
     share = [[jnp.exp(logs[i][h] - top[h]) for h in range(H)] for i in range(nlon)]
@@ -333,13 +338,11 @@
         factor = jnp.zeros((rows, D), jnp.float32)
         for h in range(H):
             factor = jnp.where(head == h, share[i][h] * total[h], factor)
-        mixed = mixed + factor * held[i, :, 0:D].astype(jnp.float32)
-    return jnp.dot(
-        mixed.astype(jnp.bfloat16), w_ref[...], preferred_element_type=jnp.float32
-    ).astype(jnp.bfloat16)
-
-
-def whole(window_bands, support_rows, state_field, conv_weight, w_query, w_key, w_value, w_out):
+        mixed = mixed + factor * held[parts[i], :, 0:D].astype(jnp.float32)
+    return mixed.astype(jnp.bfloat16)
+
+
+def whole(window_bands, support_rows, state_field, conv_weight, w_query, w_key, w_value):
     nlat, nlon = lax.axis_size("lat"), lax.axis_size("lon")
     bands = support_rows.shape[0]
     channels, high, cols = state_field.shape
@@ -354,14 +357,13 @@
     return pl.pallas_call(
         functools.partial(whole_kernel, nlat, nlon, BLOCK_KEYS),
         out_shape=jax.ShapeDtypeStruct((wide, D), half),
-        in_specs=[s, s] + [far] * 7,
+        in_specs=[s, s] + [far] * 6,
         out_specs=v,
         scratch_shapes=[
             pltpu.VMEM(conv_weight.shape, half),
-            pltpu.VMEM((D, D), half), pltpu.VMEM((D, D), half),
-            pltpu.VMEM((D, D), half), pltpu.VMEM((D, D), half),
+            pltpu.VMEM((D, D), half), pltpu.VMEM((D, D), half), pltpu.VMEM((D, D), half),
             pltpu.VMEM((total, 128), jnp.float32),
-            dma((7,)),
+            dma((6,)),
             pltpu.VMEM((total, wide, D), half),
             pltpu.VMEM((bands, wide, D), half),
             pltpu.VMEM((high + 4, cols + 16, channels), half),
@@ -381,7 +383,7 @@
         name="whole",
     )(
         window_bands, support_rows, jnp.transpose(state_field, (1, 2, 0)), conv_weight,
-        w_query, w_key, w_value, w_out, jnp.asarray(area_table(total)),
+        w_query, w_key, w_value, jnp.asarray(area_table(total)),
     )
 
 
@@ -406,9 +408,10 @@
     state_field, support_rows, window_bands, conv_weight, w_query, w_key, w_value, w_out
 ):
     lon_tile = state_field.shape[2] // 2
-    result = whole(
-        window_bands, support_rows, state_field, conv_weight, w_query, w_key, w_value, w_out
+    attended = whole(
+        window_bands, support_rows, state_field, conv_weight, w_query, w_key, w_value
     )
+    result = jnp.dot(attended, w_out, preferred_element_type=jnp.float32).astype(jnp.bfloat16)
     return result.reshape(1, lon_tile, D)
 
 

time: 80.9 us -> 78.5 us (0.970)
  Pallas kernels: 77.6 us -> 75 us
  matrix products: 0 us -> 1.53 us
  local copies, waits for them, and re-layouts: 3.16 us -> 1.82 us
    pallas_call x1, Pallas kernels: 77.6 us -> 75 us  [whole(): pl.pallas_call(functools.partial(whole_kernel, nlat, nlon, BLOCK_KEYS), o...]
    dot_general x0 -> x1, matrix products: none -> 1.53 us  [per_device(): jnp.dot(attended, w_out, preferred_element_type=jnp.float32)]
    unnamed x2 -> x3, local copies, waits for them, and re-layouts: 3.16 us -> 1.82 us
where the time goes in v5:
time: 78.5 us; the launch traced here: 78.3 us
  Pallas kernels  75 us (96%)
  local copies, waits for them, and re-layouts  1.82 us (2%)
  matrix products  1.53 us (2%)
    pallas_call x1, Pallas kernels, whole(): pl.pallas_call(functools.partial(whole_kernel, nlat, nlon, BLOCK_KEYS), o...  75 us
    unnamed x3, local copies, waits for them, and re-layouts  1.82 us

profile of v5, /device:TPU:1, one launch (start us, length us, event | category | flops | bytes accessed | tf_op | source)
XLA Modules:
  0.0 78.3 jit_solution(18313060660762560365)
XLA Ops:
  0.0 0.0 copy-start
  0.0 1.8 %copy.10 = bf16[73,8,128]{0,2,1:T(8,128)(2,1)} copy(bf16[73,8,128]{2,1,0:T(8,128)(2,1)} %param.9) | data formatting | bytes 299008 | tf_op args[0]
  1.8 75.0 %whole.1 = bf16[64,256]{1,0:T(8,128)(2,1)} custom-call(s32[32]{0:T(128)} %slot_ref.1, s32[4,5]{1,0:T(4,128)} %rows_ref.1, bf16[8,128,73]{2,1,0:T(8,128)(2,1)} %bitcast.5, bf16[5,3,73,256]{3,2,1,0:T(8,128)(2,1)} %conv_in.1, bf16[256,256]{1,0:T(8,128)(2,1)} %wq_in.1, bf16[256,256]{1,0:T(8,128)(2,1)} %wk_in.1, bf16[256,256]{1,0:T(8,128)(2,1)} %wv_in.1, ...), custom_call_target="tpu_custom_call" | custom-call | tf_op jit(solution)/shard_map/whole/pallas_call | solution.py:357
  76.8 0.0 copy-done
  76.8 1.5 %fusion = bf16[1,64,256]{2,1,0:T(8,128)(2,1)} fusion(bf16[64,256]{1,0:T(8,128)(2,1)} %whole.1, bf16[256,256]{1,0:T(8,128)(2,1)S(1)} %copy-done), kind=kOutput, calls=%fused_computation.1 | convolution fusion | flops 8404992 | bytes 196608 | tf_op jit(solution)/shard_map/dot_general | solution.py:414
Async XLA Ops:
  0.0 76.8 %copy-start = (bf16[256,256]{1,0:T(8,128)(2,1)S(1)}, bf16[256,256]{1,0:T(8,128)(2,1)}, u32[]{:S(2)}) copy-start(bf16[256,256]{1,0:T(8,128)(2,1)} %param.16) | copy-start | bytes 393220
